TPU v7x, 32 devices: a whole 2x2x4 slice. The times are simulated.
32 devices in a mesh: lev: 4 (over x, core), row: 8 (over z, y).
Axes of the slice: x: 2, y: 2, z: 4, core: 2. Of those that a mesh axis runs over, the one named last changes fastest.
Arguments:
- wind_east: float32 [16, 128, 1024], P('lev', 'row'), may hold values from -3 to 3
- wind_north: float32 [16, 128, 1024], P('lev', 'row'), may hold values from -3 to 3
- thickness: float32 [16, 128, 1024], P('lev', 'row'), may hold values from 0.5 to 2
- tracer_one: float32 [16, 128, 1024], P('lev', 'row'), may hold values from 0 to 1
- tracer_two: float32 [16, 128, 1024], P('lev', 'row'), may hold values from 0.1 to 1
- theta_step: float32 [16], replicated, may hold values from 0.5 to 2
- surface_geopot: float32 [128, 1024], P('row'), may hold values from -12 to 12
- map_factor: float32 [128, 1024], P('row'), may hold values from 0.5 to 2
- active_layers: int32 [128, 1024], P('row'), may hold values from 8 to 16
Outputs:
- east_out: float32 [16, 128, 1024], P('lev', 'row')
- north_out: float32 [16, 128, 1024], P('lev', 'row')
- thickness_out: float32 [16, 128, 1024], P('lev', 'row')
- tracer_one_out: float32 [16, 128, 1024], P('lev', 'row')
- tracer_two_out: float32 [16, 128, 1024], P('lev', 'row')
Inputs may be any that keep to these rules, and one draw needn't show every extreme that they name: Layers k with k >= active_layers of their column are below ground and keep their values.
All inputs are finite; a program needn't handle non-finite values.
Results may differ from a plain program's by a relative error of at most 0.00002.
Values sent between devices are 32-bit elements; how exact they have to be, the bound alone decides.
No kernel may reach another device: no remote copies, remote signals or barrier semaphores. Data moves between devices by JAX's collectives and lax.ppermute only.
A program may use at most 64 MiB of HBM per device.

v0:
```python
import jax
import jax.numpy as jnp
from jax import lax
from jax.sharding import PartitionSpec as P

OUTER = 2


time_step = 0.05
top_pressure = 0.1
exner_power = 2.0 / 7.0


def carried_in(part, axis, combine, identity, reverse):
    count = lax.axis_size(axis)
    place = lax.axis_index(axis)
    ahead = count - 1 - place if reverse else place
    gathered = lax.all_gather(part, axis)
    state = jnp.zeros_like(part) + jnp.asarray(identity, part.dtype)

    def one(turn, state):
        source = count - 1 - turn if reverse else turn
        return combine(state, lax.dynamic_index_in_dim(gathered, source, 0, False))

    return lax.fori_loop(0, ahead, one, state)


def extended(block, sides, width):
    for axis, dim in sides:
        count = lax.axis_size(axis)
        forward = [(i, i + 1) for i in range(count - 1)]
        forward.append((count - 1, 0))
        backward = [(target, source) for source, target in forward]
        low = lax.ppermute(
            lax.slice_in_dim(block, block.shape[dim] - width, None, axis=dim), axis, forward
        )
        high = lax.ppermute(lax.slice_in_dim(block, 0, width, axis=dim), axis, backward)
        block = jnp.concatenate([low, block, high], axis=dim)
    return block


def add_up(earlier, later):
    return earlier + later


def potential_field(mass_field, theta_own, geopot, levels):
    inside = jnp.cumsum(jnp.abs(mass_field), axis=0)
    zeros_plane = jnp.zeros(inside.shape[1:], jnp.float32)
    offset_above = carried_in(inside[-1], "lev", add_up, zeros_plane, False)
    pressure = top_pressure + (inside + offset_above[None]) / levels
    weighted = theta_own[:, None, None] * pressure**exner_power
    summed = jnp.flip(jnp.cumsum(jnp.flip(weighted, 0), axis=0), 0)
    offset_below = carried_in(summed[0], "lev", add_up, zeros_plane, True)
    return geopot[None] + (summed + offset_below[None])


def row_diff(values):
    return (values[:, 2:] - values[:, :-2]) * 0.5


def column_diff(values):
    padded = jnp.pad(values, ((0, 0), (0, 0), (1, 1)))
    return (padded[:, :, 2:] - padded[:, :, :-2]) * 0.5


def edge_diff(values):
    padded = jnp.pad(values, ((0, 0), (0, 0), (1, 1)), mode="edge")
    return (padded[:, :, 2:] - padded[:, :, :-2]) * 0.5


def tendency(padded, potential, metric, active, coriolis):
    east_wide, north_wide, mass_wide = (padded[0], padded[1], padded[2])
    east_mid = east_wide[:, 1:-1]
    north_mid = north_wide[:, 1:-1]
    metric_mid = metric[None, 1:-1]
    flux_east = mass_wide * east_wide / metric[None]
    flux_north = mass_wide[:, 1:-1] * north_mid / metric_mid
    d_mass = -(metric_mid * metric_mid) * (row_diff(flux_east) + column_diff(flux_north))

    def carried(values):
        return -metric_mid * (
            east_mid * row_diff(values) + north_mid * column_diff(values[:, 1:-1])
        )

    d_east = carried(east_wide) + coriolis * north_mid - metric_mid * row_diff(potential)
    d_north = carried(north_wide) - coriolis * east_mid - metric_mid * edge_diff(potential[:, 1:-1])
    return (
        jnp.stack([d_east, d_north, d_mass, carried(padded[3]), carried(padded[4])]) * active[None]
    )


def local(
    wind_east,
    wind_north,
    thickness,
    tracer_one,
    tracer_two,
    theta_step,
    surface_geopot,
    map_factor,
    active_layers,
):
    layers = thickness.shape[0]
    columns = thickness.shape[2]
    levels = layers * lax.axis_size("lev")
    first_layer = lax.axis_index("lev") * layers
    theta_own = lax.dynamic_slice_in_dim(theta_step, first_layer, layers)
    layer_index = first_layer + lax.broadcasted_iota(jnp.int32, (layers, 1, 1), 0)
    coriolis = 0.5 + lax.broadcasted_iota(jnp.float32, (1, columns), 1) / columns
    fields = jnp.stack([wind_east, wind_north, thickness, tracer_one, tracer_two])
    section_fractions = (1.0 / 3.0, 0.5, 1.0)
    active = (layer_index < active_layers[None]).astype(jnp.float32)
    metric = extended(map_factor, (("row", 0),), 1)
    for outer_step in range(OUTER):
        potential = potential_field(fields[2], theta_own, surface_geopot, levels)
        potential = extended(potential, (("row", 1),), 1)
        current = fields
        for fraction in section_fractions:
            padded = extended(current, (("row", 2),), 1)
            current = fields + time_step * fraction * tendency(
                padded, potential, metric, active, coriolis
            )
        fields = current
    return (fields[0], fields[1], fields[2], fields[3], fields[4])


def solution(mesh):
    placed = (
        P("lev", "row", None),
        P("lev", "row", None),
        P("lev", "row", None),
        P("lev", "row", None),
        P("lev", "row", None),
        P(),
        P("row", None),
        P("row", None),
        P("row", None),
    )
    return jax.shard_map(
        local,
        mesh=mesh,
        in_specs=placed,
        out_specs=(
            P("lev", "row", None),
            P("lev", "row", None),
            P("lev", "row", None),
            P("lev", "row", None),
            P("lev", "row", None),
        ),
        check_vma=False,
    )
```

profile of v0, /device:TPU:0, one launch (start us, length us, event | category | flops | bytes accessed | tf_op | source)
XLA Modules:
  0.0 105.4 jit_solution(11876417782226051723)
XLA Ops:
  0.6 0.8 fusion.299
  1.4 3.0 %collective-permute-start.4 = (f32[1,1024]{1,0:T(1,128)S(1)}, f32[1,1024]{1,0:T(1,128)S(1)}, u32[]{:S(2)}, u32[]{:S(2)}) collective-permute-start(f32[1,1024]{1,0:T(1,128)S(1)} %get-tuple-element.269), channel_id=1, source_target_pairs={{0,1},{1,2},{2,3},{3,4},{4,5},{5,6},{6,7},{7,0},{8,9},{9,10},{10,1... | collective-permute-start | bytes 12296 | tf_op jit(solution)/shard_map/ppermute | solution.py:34
  4.4 3.1 %collective-permute-start.5 = (f32[1,1024]{1,0:T(1,128)S(1)}, f32[1,1024]{1,0:T(1,128)S(1)}, u32[]{:S(2)}, u32[]{:S(2)}) collective-permute-start(f32[1,1024]{1,0:T(1,128)S(1)} %get-tuple-element.270), channel_id=1, source_target_pairs={{1,0},{2,1},{3,2},{4,3},{5,4},{6,5},{7,6},{0,7},{9,8},{10,9},{11,1... | collective-permute-start | bytes 12296 | tf_op jit(solution)/shard_map/ppermute | solution.py:37
  7.5 1.0 fusion.287
  8.5 5.9 %all_gather.12 = f32[4,16,1024]{2,1,0:T(8,128)S(1)} all-gather(f32[1,16,1024]{2,1,0:T(8,128)S(1)} %slice.936), channel_id=1, replica_groups=mesh['lev'=4,'row'=8] {'lev'}, dimensions={0}, use_global_device_ids=true | all-gather | bytes 327680 | tf_op jit(solution)/shard_map/all_gather | solution.py:18
  14.7 1.0 fusion.300
  15.7 6.0 %all_gather.13 = f32[4,16,1024]{2,1,0:T(8,128)S(1)} all-gather(f32[1,16,1024]{2,1,0:T(8,128)S(1)} %slice.937), channel_id=1, replica_groups=mesh['lev'=4,'row'=8] {'lev'}, dimensions={0}, use_global_device_ids=true | all-gather | bytes 327680 | tf_op jit(solution)/shard_map/all_gather | solution.py:18
  21.9 1.9 %collective-permute-start.2 = (f32[4,1,1024]{2,1,0:T(1,128)S(1)}, f32[4,1,1024]{2,1,0:T(1,128)S(1)}, u32[]{:S(2)}, u32[]{:S(2)}) collective-permute-start(f32[4,1,1024]{2,1,0:T(1,128)S(1)} %get-tuple-element.264), channel_id=1, source_target_pairs={{1,0},{2,1},{3,2},{4,3},{5,4},{6,5},{7,6},{0,7},{9,8},{10,9},{11,1... | collective-permute-start | bytes 49160 | tf_op jit(solution)/shard_map/ppermute | solution.py:37
  24.4 0.5 copy-done.1
  25.1 4.6 %collective-permute-start.1 = (f32[5,4,1,1024]{3,2,1,0:T(1,128)S(1)}, f32[5,4,1,1024]{3,2,1,0:T(1,128)S(1)}, u32[]{:S(2)}, u32[]{:S(2)}) collective-permute-start(f32[5,4,1,1024]{3,2,1,0:T(1,128)S(1)} %get-tuple-element.245), channel_id=1, source_target_pairs={{1,0},{2,1},{3,2},{4,3},{5,4},{6,5},{7,6},{0,7},{9,8},{10,9},{11,1... | collective-permute-start | bytes 245768 | tf_op jit(solution)/shard_map/ppermute | solution.py:37
  29.8 1.8 %collective-permute-done = f32[5,4,1,1024]{3,2,1,0:T(1,128)S(1)} collective-permute-done((f32[5,4,1,1024]{3,2,1,0:T(1,128)S(1)}, f32[5,4,1,1024]{3,2,1,0:T(1,128)S(1)}, u32[]{:S(2)}, u32[]{:S(2)}) %collective-permute-start) | collective-permute-done | bytes 81952 | tf_op jit(solution)/shard_map/ppermute | solution.py:34
  31.8 0.3 pad_maximum_fusion
  32.8 0.4 fusion.17
  33.9 0.3 multiply_add_fusion.5
  34.4 5.1 %collective-permute-start.7 = (f32[5,4,1,1024]{3,2,1,0:T(1,128)S(1)}, f32[5,4,1,1024]{3,2,1,0:T(1,128)S(1)}, u32[]{:S(2)}, u32[]{:S(2)}) collective-permute-start(f32[5,4,1,1024]{3,2,1,0:T(1,128)S(1)} %get-tuple-element.243), channel_id=1, source_target_pairs={{1,0},{2,1},{3,2},{4,3},{5,4},{6,5},{7,6},{0,7},{9,8},{10,9},{11,1... | collective-permute-start | bytes 245768 | tf_op jit(solution)/shard_map/ppermute | solution.py:37
  39.5 2.4 %collective-permute-done.6 = f32[5,4,1,1024]{3,2,1,0:T(1,128)S(1)} collective-permute-done((f32[5,4,1,1024]{3,2,1,0:T(1,128)S(1)}, f32[5,4,1,1024]{3,2,1,0:T(1,128)S(1)}, u32[]{:S(2)}, u32[]{:S(2)}) %collective-permute-start.6) | collective-permute-done | bytes 81952 | tf_op jit(solution)/shard_map/ppermute | solution.py:34
  41.9 0.4 pad_maximum_fusion.1
  43.0 0.4 fusion.54
  44.0 0.3 multiply_add_fusion.4
  44.3 1.1 %copy-done = f32[5,4,16,1024]{3,2,1,0:T(8,128)} copy-done((f32[5,4,16,1024]{3,2,1,0:T(8,128)}, f32[5,4,16,1024]{3,2,1,0:T(8,128)S(1)}, u32[]{:S(2)}) %copy-start) | copy-done | bytes 1310744
  45.6 4.8 %collective-permute-start.9 = (f32[5,4,1,1024]{3,2,1,0:T(1,128)S(1)}, f32[5,4,1,1024]{3,2,1,0:T(1,128)S(1)}, u32[]{:S(2)}, u32[]{:S(2)}) collective-permute-start(f32[5,4,1,1024]{3,2,1,0:T(1,128)S(1)} %get-tuple-element.241), channel_id=1, source_target_pairs={{1,0},{2,1},{3,2},{4,3},{5,4},{6,5},{7,6},{0,7},{9,8},{10,9},{11,1... | collective-permute-start | bytes 245768 | tf_op jit(solution)/shard_map/ppermute | solution.py:37
  50.5 2.4 %collective-permute-done.8 = f32[5,4,1,1024]{3,2,1,0:T(1,128)S(1)} collective-permute-done((f32[5,4,1,1024]{3,2,1,0:T(1,128)S(1)}, f32[5,4,1,1024]{3,2,1,0:T(1,128)S(1)}, u32[]{:S(2)}, u32[]{:S(2)}) %collective-permute-start.8) | collective-permute-done | bytes 81952 | tf_op jit(solution)/shard_map/ppermute | solution.py:34
  52.8 1.6 %pad_maximum_fusion.2 = f32[5,4,18,1024]{3,2,1,0:T(8,128)S(1)} fusion(f32[5,4,1,1024]{3,2,1,0:T(1,128)S(1)} %collective-permute-done.9, f32[5,4,16,1024]{3,2,1,0:T(8,128)} %copy-done, f32[5,4,1,1024]{3,2,1,0:T(1,128)S(1)} %collective-permute-done.8), kind=kLoop, calls=%fused_computation.6 | loop fusion | flops 737280 | bytes 2949120 | tf_op jit(solution)/shard_map/concatenate | solution.py:38
  55.1 0.4 fusion.91
  56.2 0.3 multiply_add_fusion.3
  56.8 4.8 %collective-permute-start.11 = (f32[5,4,1,1024]{3,2,1,0:T(1,128)S(1)}, f32[5,4,1,1024]{3,2,1,0:T(1,128)S(1)}, u32[]{:S(2)}, u32[]{:S(2)}) collective-permute-start(f32[5,4,1,1024]{3,2,1,0:T(1,128)S(1)} %get-tuple-element.239), channel_id=1, source_target_pairs={{1,0},{2,1},{3,2},{4,3},{5,4},{6,5},{7,6},{0,7},{9,8},{10,9},{11,1... | collective-permute-start | bytes 245768 | tf_op jit(solution)/shard_map/ppermute | solution.py:37
  61.7 5.8 %all_gather.14 = f32[4,16,1024]{2,1,0:T(8,128)S(1)} all-gather(f32[1,16,1024]{2,1,0:T(8,128)S(1)} %slice.1009), channel_id=1, replica_groups=mesh['lev'=4,'row'=8] {'lev'}, dimensions={0}, use_global_device_ids=true | all-gather | bytes 327680 | tf_op jit(solution)/shard_map/all_gather | solution.py:18
  67.6 1.0 fusion.301
  68.6 5.9 %all_gather.15 = f32[4,16,1024]{2,1,0:T(8,128)S(1)} all-gather(f32[1,16,1024]{2,1,0:T(8,128)S(1)} %slice.1010), channel_id=1, replica_groups=mesh['lev'=4,'row'=8] {'lev'}, dimensions={0}, use_global_device_ids=true | all-gather | bytes 327680 | tf_op jit(solution)/shard_map/all_gather | solution.py:18
  74.8 2.0 %collective-permute-start.12 = (f32[4,1,1024]{2,1,0:T(1,128)S(1)}, f32[4,1,1024]{2,1,0:T(1,128)S(1)}, u32[]{:S(2)}, u32[]{:S(2)}) collective-permute-start(f32[4,1,1024]{2,1,0:T(1,128)S(1)} %get-tuple-element.260), channel_id=1, source_target_pairs={{1,0},{2,1},{3,2},{4,3},{5,4},{6,5},{7,6},{0,7},{9,8},{10,9},{11,1... | collective-permute-start | bytes 49160 | tf_op jit(solution)/shard_map/ppermute | solution.py:37
  76.8 0.3 pad_maximum_fusion.3
  77.5 1.0 collective-permute-done.12
  78.5 4.7 %collective-permute-done.13 = f32[4,1,1024]{2,1,0:T(1,128)S(1)} collective-permute-done((f32[4,1,1024]{2,1,0:T(1,128)S(1)}, f32[4,1,1024]{2,1,0:T(1,128)S(1)}, u32[]{:S(2)}, u32[]{:S(2)}) %collective-permute-start.13) | collective-permute-done | bytes 16416 | tf_op jit(solution)/shard_map/ppermute | solution.py:34
  83.2 0.3 fusion.119
  83.5 0.4 fusion.128
  84.5 0.3 multiply_add_fusion.2
  85.0 4.7 %collective-permute-start.15 = (f32[5,4,1,1024]{3,2,1,0:T(1,128)S(1)}, f32[5,4,1,1024]{3,2,1,0:T(1,128)S(1)}, u32[]{:S(2)}, u32[]{:S(2)}) collective-permute-start(f32[5,4,1,1024]{3,2,1,0:T(1,128)S(1)} %get-tuple-element.237), channel_id=1, source_target_pairs={{1,0},{2,1},{3,2},{4,3},{5,4},{6,5},{7,6},{0,7},{9,8},{10,9},{11,1... | collective-permute-start | bytes 245768 | tf_op jit(solution)/shard_map/ppermute | solution.py:37
  89.7 2.4 %collective-permute-done.14 = f32[5,4,1,1024]{3,2,1,0:T(1,128)S(1)} collective-permute-done((f32[5,4,1,1024]{3,2,1,0:T(1,128)S(1)}, f32[5,4,1,1024]{3,2,1,0:T(1,128)S(1)}, u32[]{:S(2)}, u32[]{:S(2)}) %collective-permute-start.14) | collective-permute-done | bytes 81952 | tf_op jit(solution)/shard_map/ppermute | solution.py:34
  92.1 0.4 pad_maximum_fusion.4
  92.9 0.3 fusion.156
  93.2 0.4 fusion.165
  94.2 0.3 multiply_add_fusion.1
  94.8 4.8 %collective-permute-start.17 = (f32[5,4,1,1024]{3,2,1,0:T(1,128)S(1)}, f32[5,4,1,1024]{3,2,1,0:T(1,128)S(1)}, u32[]{:S(2)}, u32[]{:S(2)}) collective-permute-start(f32[5,4,1,1024]{3,2,1,0:T(1,128)S(1)} %get-tuple-element.235), channel_id=1, source_target_pairs={{1,0},{2,1},{3,2},{4,3},{5,4},{6,5},{7,6},{0,7},{9,8},{10,9},{11,1... | collective-permute-start | bytes 245768 | tf_op jit(solution)/shard_map/ppermute | solution.py:37
  99.5 2.4 %collective-permute-done.16 = f32[5,4,1,1024]{3,2,1,0:T(1,128)S(1)} collective-permute-done((f32[5,4,1,1024]{3,2,1,0:T(1,128)S(1)}, f32[5,4,1,1024]{3,2,1,0:T(1,128)S(1)}, u32[]{:S(2)}, u32[]{:S(2)}) %collective-permute-start.16) | collective-permute-done | bytes 81952 | tf_op jit(solution)/shard_map/ppermute | solution.py:34
  101.9 0.4 pad_maximum_fusion.5
  103.0 0.4 fusion.202
  104.0 0.3 multiply_add_fusion
  104.3 1.1 %slice_bitcast_fusion.30 = (f32[4,16,1024]{2,1,0:T(8,128)}, f32[4,16,1024]{2,1,0:T(8,128)}, f32[4,16,1024]{2,1,0:T(8,128)}, f32[4,16,1024]{2,1,0:T(8,128)}, f32[4,16,1024]{2,1,0:T(8,128)}) fusion(f32[5,4,16,1024]{3,2,1,0:T(8,128)S(1)} %multiply_add_fusion), kind=kLoop, calls=%fused_computation.334 | loop fusion | bytes 2621440 | tf_op jit(solution)/shard_map/squeeze | solution.py:124
  (141 shorter events, 10.3 us)
Async XLA Ops:
  0.6 13.7 %copy-start.9 = (f32[16]{0:T(128)S(1)}, f32[16]{0:T(128)}, u32[]{:S(2)}) copy-start(f32[16]{0:T(128)} %param.22) | copy-start | bytes 196
  1.4 23.7 %collective-permute-start.4 = (f32[1,1024]{1,0:T(1,128)S(1)}, f32[1,1024]{1,0:T(1,128)S(1)}, u32[]{:S(2)}, u32[]{:S(2)}) collective-permute-start(f32[1,1024]{1,0:T(1,128)S(1)} %get-tuple-element.269), channel_id=1, source_target_pairs={{0,1},{1,2},{2,3},{3,4},{4,5},{5,6},{6,7},{7,0},{8,9},{9,10},{10,1... | collective-permute-start | bytes 12296 | tf_op jit(solution)/shard_map/ppermute | solution.py:34
  4.4 25.3 %collective-permute-start.5 = (f32[1,1024]{1,0:T(1,128)S(1)}, f32[1,1024]{1,0:T(1,128)S(1)}, u32[]{:S(2)}, u32[]{:S(2)}) collective-permute-start(f32[1,1024]{1,0:T(1,128)S(1)} %get-tuple-element.270), channel_id=1, source_target_pairs={{1,0},{2,1},{3,2},{4,3},{5,4},{6,5},{7,6},{0,7},{9,8},{10,9},{11,1... | collective-permute-start | bytes 12296 | tf_op jit(solution)/shard_map/ppermute | solution.py:37
  14.6 7.2 %copy-start.3 = (f32[16,1024]{1,0:T(8,128)S(1)}, f32[16,1024]{1,0:T(8,128)}, u32[]{:S(2)}) copy-start(f32[16,1024]{1,0:T(8,128)} %param.23) | copy-start | bytes 196612
  15.7 8.4 %copy-start.4 = (f32[4,16,1024]{2,1,0:T(8,128)S(1)}, f32[4,16,1024]{2,1,0:T(8,128)}, u32[]{:S(2)}) copy-start(f32[4,16,1024]{2,1,0:T(8,128)} %param.17) | copy-start | bytes 786436
  21.7 2.4 %copy-start.5 = (f32[4,16,1024]{2,1,0:T(8,128)S(1)}, f32[4,16,1024]{2,1,0:T(8,128)}, u32[]{:S(2)}) copy-start(f32[4,16,1024]{2,1,0:T(8,128)} %param.18) | copy-start | bytes 786436
  21.7 2.4 %copy-start.2 = (f32[4,16,1024]{2,1,0:T(8,128)S(1)}, f32[4,16,1024]{2,1,0:T(8,128)}, u32[]{:S(2)}) copy-start(f32[4,16,1024]{2,1,0:T(8,128)} %param.19) | copy-start | bytes 786436
  21.8 2.3 %copy-start.6 = (f32[4,16,1024]{2,1,0:T(8,128)S(1)}, f32[4,16,1024]{2,1,0:T(8,128)}, u32[]{:S(2)}) copy-start(f32[4,16,1024]{2,1,0:T(8,128)} %param.20) | copy-start | bytes 786436
  21.9 2.3 %copy-start.7 = (f32[4,16,1024]{2,1,0:T(8,128)S(1)}, f32[4,16,1024]{2,1,0:T(8,128)}, u32[]{:S(2)}) copy-start(f32[4,16,1024]{2,1,0:T(8,128)} %param.21) | copy-start | bytes 786436
  21.9 10.6 %collective-permute-start.2 = (f32[4,1,1024]{2,1,0:T(1,128)S(1)}, f32[4,1,1024]{2,1,0:T(1,128)S(1)}, u32[]{:S(2)}, u32[]{:S(2)}) collective-permute-start(f32[4,1,1024]{2,1,0:T(1,128)S(1)} %get-tuple-element.264), channel_id=1, source_target_pairs={{1,0},{2,1},{3,2},{4,3},{5,4},{6,5},{7,6},{0,7},{9,8},{10,9},{11,1... | collective-permute-start | bytes 49160 | tf_op jit(solution)/shard_map/ppermute | solution.py:37
  23.9 8.7 %collective-permute-start.3 = (f32[4,1,1024]{2,1,0:T(1,128)S(1)}, f32[4,1,1024]{2,1,0:T(1,128)S(1)}, u32[]{:S(2)}, u32[]{:S(2)}) collective-permute-start(f32[4,1,1024]{2,1,0:T(1,128)S(1)} %get-tuple-element.265), channel_id=1, source_target_pairs={{0,1},{1,2},{2,3},{3,4},{4,5},{5,6},{6,7},{7,0},{8,9},{9,10},{10,1... | collective-permute-start | bytes 49160 | tf_op jit(solution)/shard_map/ppermute | solution.py:34
  24.1 0.8 copy-start.1
  24.1 0.9 copy-start.8
  24.4 7.2 %collective-permute-start = (f32[5,4,1,1024]{3,2,1,0:T(1,128)S(1)}, f32[5,4,1,1024]{3,2,1,0:T(1,128)S(1)}, u32[]{:S(2)}, u32[]{:S(2)}) collective-permute-start(f32[5,4,1,1024]{3,2,1,0:T(1,128)S(1)} %get-tuple-element.244), channel_id=1, source_target_pairs={{0,1},{1,2},{2,3},{3,4},{4,5},{5,6},{6,7},{7,0},{8,9},{9,10},{10,1... | collective-permute-start | bytes 245768 | tf_op jit(solution)/shard_map/ppermute | solution.py:34
  25.1 6.7 %collective-permute-start.1 = (f32[5,4,1,1024]{3,2,1,0:T(1,128)S(1)}, f32[5,4,1,1024]{3,2,1,0:T(1,128)S(1)}, u32[]{:S(2)}, u32[]{:S(2)}) collective-permute-start(f32[5,4,1,1024]{3,2,1,0:T(1,128)S(1)} %get-tuple-element.245), channel_id=1, source_target_pairs={{1,0},{2,1},{3,2},{4,3},{5,4},{6,5},{7,6},{0,7},{9,8},{10,9},{11,1... | collective-permute-start | bytes 245768 | tf_op jit(solution)/shard_map/ppermute | solution.py:37
  34.3 7.6 %collective-permute-start.6 = (f32[5,4,1,1024]{3,2,1,0:T(1,128)S(1)}, f32[5,4,1,1024]{3,2,1,0:T(1,128)S(1)}, u32[]{:S(2)}, u32[]{:S(2)}) collective-permute-start(f32[5,4,1,1024]{3,2,1,0:T(1,128)S(1)} %get-tuple-element.242), channel_id=1, source_target_pairs={{0,1},{1,2},{2,3},{3,4},{4,5},{5,6},{6,7},{7,0},{8,9},{9,10},{10,1... | collective-permute-start | bytes 245768 | tf_op jit(solution)/shard_map/ppermute | solution.py:34
  34.4 7.5 %collective-permute-start.7 = (f32[5,4,1,1024]{3,2,1,0:T(1,128)S(1)}, f32[5,4,1,1024]{3,2,1,0:T(1,128)S(1)}, u32[]{:S(2)}, u32[]{:S(2)}) collective-permute-start(f32[5,4,1,1024]{3,2,1,0:T(1,128)S(1)} %get-tuple-element.243), channel_id=1, source_target_pairs={{1,0},{2,1},{3,2},{4,3},{5,4},{6,5},{7,6},{0,7},{9,8},{10,9},{11,1... | collective-permute-start | bytes 245768 | tf_op jit(solution)/shard_map/ppermute | solution.py:37
  44.3 1.1 %copy-start = (f32[5,4,16,1024]{3,2,1,0:T(8,128)}, f32[5,4,16,1024]{3,2,1,0:T(8,128)S(1)}, u32[]{:S(2)}) copy-start(f32[5,4,16,1024]{3,2,1,0:T(8,128)S(1)} %multiply_add_fusion.4) | copy-start | bytes 3932164
  45.6 7.3 %collective-permute-start.8 = (f32[5,4,1,1024]{3,2,1,0:T(1,128)S(1)}, f32[5,4,1,1024]{3,2,1,0:T(1,128)S(1)}, u32[]{:S(2)}, u32[]{:S(2)}) collective-permute-start(f32[5,4,1,1024]{3,2,1,0:T(1,128)S(1)} %get-tuple-element.240), channel_id=1, source_target_pairs={{0,1},{1,2},{2,3},{3,4},{4,5},{5,6},{6,7},{7,0},{8,9},{9,10},{10,1... | collective-permute-start | bytes 245768 | tf_op jit(solution)/shard_map/ppermute | solution.py:34
  45.6 7.2 %collective-permute-start.9 = (f32[5,4,1,1024]{3,2,1,0:T(1,128)S(1)}, f32[5,4,1,1024]{3,2,1,0:T(1,128)S(1)}, u32[]{:S(2)}, u32[]{:S(2)}) collective-permute-start(f32[5,4,1,1024]{3,2,1,0:T(1,128)S(1)} %get-tuple-element.241), channel_id=1, source_target_pairs={{1,0},{2,1},{3,2},{4,3},{5,4},{6,5},{7,6},{0,7},{9,8},{10,9},{11,1... | collective-permute-start | bytes 245768 | tf_op jit(solution)/shard_map/ppermute | solution.py:37
  56.8 20.0 %collective-permute-start.10 = (f32[5,4,1,1024]{3,2,1,0:T(1,128)S(1)}, f32[5,4,1,1024]{3,2,1,0:T(1,128)S(1)}, u32[]{:S(2)}, u32[]{:S(2)}) collective-permute-start(f32[5,4,1,1024]{3,2,1,0:T(1,128)S(1)} %get-tuple-element.238), channel_id=1, source_target_pairs={{0,1},{1,2},{2,3},{3,4},{4,5},{5,6},{6,7},{7,0},{8,9},{9,10},{10,1... | collective-permute-start | bytes 245768 | tf_op jit(solution)/shard_map/ppermute | solution.py:34
  56.8 20.0 %collective-permute-start.11 = (f32[5,4,1,1024]{3,2,1,0:T(1,128)S(1)}, f32[5,4,1,1024]{3,2,1,0:T(1,128)S(1)}, u32[]{:S(2)}, u32[]{:S(2)}) collective-permute-start(f32[5,4,1,1024]{3,2,1,0:T(1,128)S(1)} %get-tuple-element.239), channel_id=1, source_target_pairs={{1,0},{2,1},{3,2},{4,3},{5,4},{6,5},{7,6},{0,7},{9,8},{10,9},{11,1... | collective-permute-start | bytes 245768 | tf_op jit(solution)/shard_map/ppermute | solution.py:37
  74.8 3.7 %collective-permute-start.12 = (f32[4,1,1024]{2,1,0:T(1,128)S(1)}, f32[4,1,1024]{2,1,0:T(1,128)S(1)}, u32[]{:S(2)}, u32[]{:S(2)}) collective-permute-start(f32[4,1,1024]{2,1,0:T(1,128)S(1)} %get-tuple-element.260), channel_id=1, source_target_pairs={{1,0},{2,1},{3,2},{4,3},{5,4},{6,5},{7,6},{0,7},{9,8},{10,9},{11,1... | collective-permute-start | bytes 49160 | tf_op jit(solution)/shard_map/ppermute | solution.py:37
  76.8 6.4 %collective-permute-start.13 = (f32[4,1,1024]{2,1,0:T(1,128)S(1)}, f32[4,1,1024]{2,1,0:T(1,128)S(1)}, u32[]{:S(2)}, u32[]{:S(2)}) collective-permute-start(f32[4,1,1024]{2,1,0:T(1,128)S(1)} %get-tuple-element.261), channel_id=1, source_target_pairs={{0,1},{1,2},{2,3},{3,4},{4,5},{5,6},{6,7},{7,0},{8,9},{9,10},{10,1... | collective-permute-start | bytes 49160 | tf_op jit(solution)/shard_map/ppermute | solution.py:34
  84.9 7.2 %collective-permute-start.14 = (f32[5,4,1,1024]{3,2,1,0:T(1,128)S(1)}, f32[5,4,1,1024]{3,2,1,0:T(1,128)S(1)}, u32[]{:S(2)}, u32[]{:S(2)}) collective-permute-start(f32[5,4,1,1024]{3,2,1,0:T(1,128)S(1)} %get-tuple-element.236), channel_id=1, source_target_pairs={{0,1},{1,2},{2,3},{3,4},{4,5},{5,6},{6,7},{7,0},{8,9},{9,10},{10,1... | collective-permute-start | bytes 245768 | tf_op jit(solution)/shard_map/ppermute | solution.py:34
  85.0 7.1 %collective-permute-start.15 = (f32[5,4,1,1024]{3,2,1,0:T(1,128)S(1)}, f32[5,4,1,1024]{3,2,1,0:T(1,128)S(1)}, u32[]{:S(2)}, u32[]{:S(2)}) collective-permute-start(f32[5,4,1,1024]{3,2,1,0:T(1,128)S(1)} %get-tuple-element.237), channel_id=1, source_target_pairs={{1,0},{2,1},{3,2},{4,3},{5,4},{6,5},{7,6},{0,7},{9,8},{10,9},{11,1... | collective-permute-start | bytes 245768 | tf_op jit(solution)/shard_map/ppermute | solution.py:37
  94.7 7.2 %collective-permute-start.16 = (f32[5,4,1,1024]{3,2,1,0:T(1,128)S(1)}, f32[5,4,1,1024]{3,2,1,0:T(1,128)S(1)}, u32[]{:S(2)}, u32[]{:S(2)}) collective-permute-start(f32[5,4,1,1024]{3,2,1,0:T(1,128)S(1)} %get-tuple-element.234), channel_id=1, source_target_pairs={{0,1},{1,2},{2,3},{3,4},{4,5},{5,6},{6,7},{7,0},{8,9},{9,10},{10,1... | collective-permute-start | bytes 245768 | tf_op jit(solution)/shard_map/ppermute | solution.py:34
  94.8 7.1 %collective-permute-start.17 = (f32[5,4,1,1024]{3,2,1,0:T(1,128)S(1)}, f32[5,4,1,1024]{3,2,1,0:T(1,128)S(1)}, u32[]{:S(2)}, u32[]{:S(2)}) collective-permute-start(f32[5,4,1,1024]{3,2,1,0:T(1,128)S(1)} %get-tuple-element.235), channel_id=1, source_target_pairs={{1,0},{2,1},{3,2},{4,3},{5,4},{6,5},{7,6},{0,7},{9,8},{10,9},{11,1... | collective-permute-start | bytes 245768 | tf_op jit(solution)/shard_map/ppermute | solution.py:37
where the time goes:
time: 106 us; the launch traced here: 105 us
  starting transfers between devices  39.5 us (37%)
  blocking collectives  23.5 us (22%)
  other arithmetic  17.5 us (17%)
  waiting for transfers between devices  17.2 us (16%)
  local copies, waits for them, and re-layouts  6.07 us (6%)
  between operations  1.51 us (1%)
    ppermute x9, starting transfers between devices, extended(): lax.ppermute(lax.slice_in_dim(block, 0, width, axis=dim), axis, backward)  35.9 us
    all_gather x4, blocking collectives, carried_in(): gathered = lax.all_gather(part, axis)  23.5 us
    ppermute x9, waiting for transfers between devices, extended(): lax.ppermute(lax.slice_in_dim(block, block.shape[dim] - width, None, axis...  15.9 us
    unnamed x24, other arithmetic  6.39 us
    ppermute x9, starting transfers between devices, extended(): lax.ppermute(lax.slice_in_dim(block, block.shape[dim] - width, None, axis...  3.54 us
    concatenate x7, other arithmetic, extended(): block = jnp.concatenate([low, block, high], axis=dim)  3.45 us
  transfers between devices with their start and end apart: 18, of which 8 were waited for; matrix products, arithmetic and copies ran while one was open for 5% of the time, Pallas kernels for 0%

commit v1 on v0

v1 whole, which is shorter than its diff:
```python
import functools

import jax
import jax.numpy as jnp
from jax import lax
from jax.experimental import pallas as pl
from jax.experimental.pallas import tpu as pltpu
from jax.sharding import PartitionSpec as P

OUTER = 2
FRACTIONS = (1.0 / 3.0, 0.5, 1.0)
LANES = 128

time_step = 0.05
top_pressure = 0.1
exner_power = 2.0 / 7.0

VMEM = pl.BlockSpec(memory_space=pltpu.VMEM)
SMEM = pl.BlockSpec(memory_space=pltpu.SMEM)
ANY = pl.BlockSpec(memory_space=pl.ANY)


class Geometry:
    def __init__(self, layers, rows, columns, levels):
        self.layers, self.rows, self.columns, self.levels = layers, rows, columns, levels
        self.sub = 2 * layers
        self.tiles = columns // LANES
        self.halo = OUTER * len(FRACTIONS)
        self.wide = rows + 2 * self.halo
        self.margin = 8
        self.plane = rows + 2 * self.margin
        assert self.sub == 8 and columns % LANES == 0 and rows % 8 == 0
        assert self.halo % 2 == 0 and self.halo <= self.margin <= rows


def lane(c):
    return pl.ds(c * LANES, LANES)


def sublane_index(g):
    return lax.broadcasted_iota(jnp.int32, (g.sub, LANES), 0)


def top_half(g):
    return sublane_index(g) < g.layers


def swap_halves(g, value):
    return pltpu.roll(value, g.layers, 0)


def column_differences(g, values, edge):
    lanes = lax.broadcasted_iota(jnp.int32, (g.sub, LANES), 1)
    first, last = lanes == 0, lanes == LANES - 1
    right_moved = [pltpu.roll(v, 1, 1) for v in values]
    left_moved = [pltpu.roll(v, LANES - 1, 1) for v in values]
    zero = jnp.zeros((g.sub, LANES), jnp.float32)
    result = []
    for c in range(g.tiles):
        before = right_moved[c - 1] if c > 0 else (values[c] if edge else zero)
        after = left_moved[c + 1] if c < g.tiles - 1 else (values[c] if edge else zero)
        result.append(
            jnp.where(last, after, left_moved[c]) - jnp.where(first, before, right_moved[c])
        )
    return result


def row_of(g, ref, e):
    return [ref[e, :, lane(c)] for c in range(g.tiles)]


def spread(flat, height, c, row):
    return flat[pl.ds(c * height + row, 8, stride=0), :]


def copy_fields(g, fields, scratch, sem):
    copies = []
    for slot, field in enumerate(fields):
        for c in range(g.tiles):
            copies.append(
                pltpu.make_async_copy(field.at[:, :, lane(c)], scratch.at[c, slot], sem)
            )
    return copies


def pack_kernel(g, u, v, h, q1, q2, metric, active, geopot,
                up, down, late_up, late_down, uv, hh, qq, mass, s_uv, s_hh, s_qq, sem):
    copies = (copy_fields(g, (h, h), s_hh, sem.at[0]) + copy_fields(g, (u, v), s_uv, sem.at[0])
              + copy_fields(g, (q1, q2), s_qq, sem.at[0]))
    for one in copies:
        one.start()
    for one in copies:
        one.wait()
    for c in range(g.tiles):
        total = jnp.abs(s_hh[c, 0, 0])
        for k in range(1, g.layers):
            total = total + jnp.abs(s_hh[c, 0, k])
        mass[:, lane(c)] = total
    block = g.sub * g.rows

    for source, target in ((s_uv, uv), (s_hh, hh), (s_qq, qq)):
        flat = source.reshape(g.tiles * block, LANES)

        def one_row(r, carry, flat=flat, target=target):
            for c in range(g.tiles):
                target[r, :, lane(c)] = flat[pl.ds(c * block + r, g.sub, stride=g.rows), :]
            return carry

        lax.fori_loop(0, g.rows, one_row, 0)
    top = top_half(g)
    n = g.halo
    for out, late, start, edge in ((up, late_up, g.rows - n, g.rows - g.margin),
                                   (down, late_down, 0, 0)):
        for c in range(g.tiles):
            for i in range(n):
                out[i, :, lane(c)] = uv[start + i, :, lane(c)]
                late[i, :, lane(c)] = qq[start + i, :, lane(c)]
            for i in range(n // 2):
                out[n + i, :, lane(c)] = jnp.where(
                    top, hh[start + 2 * i, :, lane(c)], hh[start + 2 * i + 1, :, lane(c)])
            span = pl.ds(edge, g.margin)
            out[n + n // 2, :, lane(c)] = metric[span, lane(c)]
            out[n + n // 2 + 1, :, lane(c)] = active[span, lane(c)].astype(jnp.float32)
            late[n, :, lane(c)] = geopot[span, lane(c)]


def exner_kernel(g, place, theta, h, gathered, weighted, below):
    me = place[0]
    count = gathered.shape[0]
    for c in range(g.tiles):
        running = jnp.zeros((g.rows, LANES), jnp.float32)
        for other in range(count):
            running = running + gathered[other, :, lane(c)] * jnp.where(other < me, 1.0, 0.0)
        terms = []
        for k in range(g.layers):
            running = running + jnp.abs(h[k, :, lane(c)])
            pressure = top_pressure + running * (1.0 / g.levels)
            terms.append(theta[me * g.layers + k] * jnp.exp(exner_power * jnp.log(pressure)))
        for k in range(g.layers - 2, -1, -1):
            terms[k] = terms[k] + terms[k + 1]
        for k in range(g.layers):
            weighted[k, :, lane(c)] = terms[k]
        below[:, lane(c)] = terms[0]


def montgomery_kernel(g, place, weighted, gathered, geopot, up, down, mm, s_mm):
    me = place[0]
    count = gathered.shape[0]
    block = g.sub * g.rows
    for c in range(g.tiles):
        offset = jnp.zeros((g.rows, LANES), jnp.float32)
        for other in range(count):
            offset = offset + gathered[other, :, lane(c)] * jnp.where(other > me, 1.0, 0.0)
        for k in range(g.layers):
            value = geopot[:, lane(c)] + (weighted[k, :, lane(c)] + offset)
            s_mm[c, 0, k] = value
            s_mm[c, 1, k] = value
    flat = s_mm.reshape(g.tiles * block, LANES)

    def one_row(r, carry):
        for c in range(g.tiles):
            mm[r, :, lane(c)] = flat[pl.ds(c * block + r, g.sub, stride=g.rows), :]
        return carry

    lax.fori_loop(0, g.rows, one_row, 0)
    top = top_half(g)
    for out, start in ((up, g.rows - g.halo), (down, 0)):
        for c in range(g.tiles):
            for i in range(g.halo // 2):
                out[i, :, lane(c)] = jnp.where(
                    top, mm[start + 2 * i, :, lane(c)], mm[start + 2 * i + 1, :, lane(c)])


def unpack_pair(g, top, value):
    other = swap_halves(g, value)
    return jnp.where(top, value, other), jnp.where(top, other, value)


def fill_planes(g, up, down, metric, active, s_metric, s_inverse, s_active):
    n = g.halo + g.halo // 2
    low, high = pl.ds(0, g.margin), pl.ds(g.margin + g.rows, g.margin)
    own = pl.ds(g.margin, g.rows)
    for c in range(g.tiles):
        for span, value, count in (
            (low, up[n, :, lane(c)], up[n + 1, :, lane(c)]),
            (own, metric[:, lane(c)], active[:, lane(c)].astype(jnp.float32)),
            (high, down[n, :, lane(c)], down[n + 1, :, lane(c)]),
        ):
            s_metric[c, span] = value
            s_inverse[c, span] = 1.0 / value
            s_active[c, span] = count


class Planes:
    def __init__(self, g, place, s_metric, s_inverse, s_active):
        self.g = g
        flat = lambda ref: ref.reshape(g.tiles * g.plane, LANES)
        self.metric_rows, self.inverse_rows = flat(s_metric), flat(s_inverse)
        self.active_rows = flat(s_active)
        self.shift = g.margin - g.halo
        layer = place[0] * g.layers + lax.rem(sublane_index(g), g.layers)
        self.layer = layer.astype(jnp.float32)

    def metric(self, e, c):
        return spread(self.metric_rows, self.g.plane, c, e + self.shift)

    def inverse(self, e, c):
        return spread(self.inverse_rows, self.g.plane, c, e + self.shift)

    def active(self, e, c, scale):
        count = spread(self.active_rows, self.g.plane, c, e + self.shift)
        return jnp.where(self.layer < count, scale, 0.0)


def signed_coriolis(g, c):
    column = (lax.broadcasted_iota(jnp.int32, (g.sub, LANES), 1) + c * LANES).astype(jnp.float32)
    f = 0.5 + column / g.columns
    return jnp.where(top_half(g), f, -f)


def section(g, planes, low, high, scale, uv, uv0, mass=None, tracer=None):
    top = top_half(g)

    def put(target, e, c, value):
        if target is None:
            return
        if callable(target):
            target(e, c, value)
        else:
            target[e, :, lane(c)] = value

    def one_row(e, carry):
        here = row_of(g, uv, e)
        if mass is not None:
            flux, hh0, gradient, coriolis, uv_out, flux_out, hh_out = mass
            uv_columns = column_differences(g, here, False)
            flux_columns = column_differences(g, row_of(g, flux, e), False)
        if tracer is not None:
            qq, qq0, qq_out = tracer
            qq_columns = column_differences(g, row_of(g, qq, e), False)
        for c in range(g.tiles):
            swapped = swap_halves(g, here[c])
            east = jnp.where(top, here[c], swapped)
            north = jnp.where(top, swapped, here[c])
            metric = planes.metric(e, c)
            live = planes.active(e, c, scale)
            carry_scale = live * (metric * -0.5)
            if tracer is not None:
                rows = qq[e + 1, :, lane(c)] - qq[e - 1, :, lane(c)]
                put(qq_out, e, c, qq0[e, :, lane(c)]
                    + carry_scale * (east * rows + north * qq_columns[c]))
            if mass is not None:
                rows = uv[e + 1, :, lane(c)] - uv[e - 1, :, lane(c)]
                uv_new = (uv0[e, :, lane(c)]
                          + carry_scale * (east * rows + north * uv_columns[c]
                                           + gradient[e, :, lane(c)])
                          + live * (coriolis[:, lane(c)] * swapped))
                put(uv_out, e, c, uv_new)
                rows = flux[e + 1, :, lane(c)] - flux[e - 1, :, lane(c)]
                mixed = jnp.where(top, rows, flux_columns[c])
                hh_new = hh0[e, :, lane(c)] + (carry_scale * metric) * (
                    mixed + swap_halves(g, mixed))
                put(hh_out, e, c, hh_new)
                if flux_out is not None:
                    put(flux_out, e, c, hh_new * uv_new * planes.inverse(e, c))
        return carry

    lax.fori_loop(low, high, one_row, 0)


def fill_flux(g, planes, low, high, uv, hh, flux):
    def one_row(e, carry):
        for c in range(g.tiles):
            flux[e, :, lane(c)] = (
                hh[e, :, lane(c)] * uv[e, :, lane(c)] * planes.inverse(e, c))
        return carry

    lax.fori_loop(low, high, one_row, 0)


def fill_gradient(g, low, high, mm, gradient):
    top = top_half(g)

    def one_row(e, carry):
        columns = column_differences(g, row_of(g, mm, e), True)
        for c in range(g.tiles):
            gradient[e, :, lane(c)] = jnp.where(
                top, mm[e + 1, :, lane(c)] - mm[e - 1, :, lane(c)], columns[c])
        return carry

    lax.fori_loop(low, high, one_row, 0)


def fill_coriolis(g, coriolis):
    for c in range(g.tiles):
        coriolis[:, lane(c)] = signed_coriolis(g, c)


def first_step_kernel(g, place, uv_own, hh_own, mm_own, up, down, m_up, m_down, metric, active,
                      uv0, uv1, uv2, uv3, hh3, mass,
                      hh0, mm, flux0, flux1, gradient, coriolis,
                      s_metric, s_inverse, s_active, sem):
    n = g.halo
    own = pl.ds(n, g.rows)
    copies = [
        pltpu.make_async_copy(uv_own, uv0.at[own], sem.at[0]),
        pltpu.make_async_copy(hh_own, hh0.at[own], sem.at[1]),
        pltpu.make_async_copy(mm_own, mm.at[own], sem.at[2]),
    ]
    for one in copies:
        one.start()
    fill_planes(g, up, down, metric, active, s_metric, s_inverse, s_active)
    fill_coriolis(g, coriolis)
    planes = Planes(g, place, s_metric, s_inverse, s_active)
    top = top_half(g)
    for halo, m_halo, start in ((up, m_up, 0), (down, m_down, n + g.rows)):
        for c in range(g.tiles):
            for i in range(n):
                uv0[start + i, :, lane(c)] = halo[i, :, lane(c)]
            for i in range(n // 2):
                for target, source in ((hh0, halo[n + i, :, lane(c)]),
                                       (mm, m_halo[i, :, lane(c)])):
                    one, two = unpack_pair(g, top, source)
                    target[start + 2 * i, :, lane(c)] = one
                    target[start + 2 * i + 1, :, lane(c)] = two
    for one in copies:
        one.wait()
    w = g.wide
    fill_flux(g, planes, 0, w, uv0, hh0, flux0)
    fill_gradient(g, 1, w - 1, mm, gradient)
    s = [time_step * fraction for fraction in FRACTIONS]
    section(g, planes, 1, w - 1, s[0], uv0, uv0,
            mass=(flux0, hh0, gradient, coriolis, uv1, flux1, None))
    section(g, planes, 2, w - 2, s[1], uv1, uv0,
            mass=(flux1, hh0, gradient, coriolis, uv2, flux0, None))
    first = len(FRACTIONS)

    section(g, planes, first, w - first, s[2], uv2, uv0,
            mass=(flux0, hh0, gradient, coriolis, uv3, None, hh3))
    fill_mass(g, first, w - first, hh3, mass)


def any_lane(c):
    return pl.ds(pl.multiple_of(c * LANES, LANES), LANES)


def fill_mass(g, low, high, hh, mass):
    place_in = sublane_index(g)

    def one_tile(c, carry):
        for start in range(0, mass.shape[0], g.sub):
            rows = jnp.zeros((g.sub, LANES), jnp.float32)
            for j in range(g.sub):
                e = low + start + j
                if e < high:
                    size = jnp.abs(hh[e, :, any_lane(c)])
                    size = size + pltpu.roll(size, 1, 0)
                    size = size + pltpu.roll(size, 2, 0)
                    rows = jnp.where(place_in == j, size, rows)
            mass[pl.ds(start, g.sub), any_lane(c)] = rows
        return carry

    lax.fori_loop(0, g.tiles, one_tile, 0)


def second_exner_kernel(g, place, theta, hh, gathered, weighted, below, s_offset):
    me = place[0]
    count = gathered.shape[0]
    height = s_offset.shape[1]
    for c in range(g.tiles):
        offset = jnp.zeros((height, LANES), jnp.float32)
        for other in range(count):
            offset = offset + gathered[other, :, lane(c)] * jnp.where(other < me, 1.0, 0.0)
        s_offset[c] = offset
    flat = s_offset.reshape(g.tiles * height, LANES)
    top = top_half(g)
    layer = lax.rem(sublane_index(g), g.layers)
    first = len(FRACTIONS)
    jump = jnp.zeros((g.sub, LANES), jnp.float32)
    for k in range(g.layers):
        jump = jnp.where(layer == k, theta[me * g.layers + k], jump)

    place_in = sublane_index(g)
    pairs = (g.wide - 2 * first) // 2

    def one_tile(c, carry):
        for start in range(0, height, g.sub):
            rows = jnp.zeros((g.sub, LANES), jnp.float32)
            for j in range(0, g.sub, 2):
                i = (start + j) // 2
                if i >= pairs:
                    continue
                e = first + 2 * i
                size = jnp.abs(jnp.where(top, hh[e, :, any_lane(c)], hh[e + 1, :, any_lane(c)]))
                size = size + jnp.where(layer >= 1, pltpu.roll(size, 1, 0), 0.0)
                size = size + jnp.where(layer >= 2, pltpu.roll(size, 2, 0), 0.0)
                offset = jnp.where(top, spread(flat, height, c, 2 * i),
                                   spread(flat, height, c, 2 * i + 1))
                pressure = top_pressure + (size + offset) * (1.0 / g.levels)
                term = jump * jnp.exp(exner_power * jnp.log(pressure))
                term = term + jnp.where(
                    layer < g.layers - 1, pltpu.roll(term, g.sub - 1, 0), 0.0)
                term = term + jnp.where(
                    layer < g.layers - 2, pltpu.roll(term, g.sub - 2, 0), 0.0)
                weighted[i, :, any_lane(c)] = term
                first_row = pltpu.roll(term, j, 0) if j else term
                rows = jnp.where(place_in == j, first_row, rows)
                rows = jnp.where(
                    place_in == j + 1, pltpu.roll(term, (j + 1 - g.layers) % g.sub, 0), rows)
            below[pl.ds(start, g.sub), any_lane(c)] = rows
        return carry

    lax.fori_loop(0, g.tiles, one_tile, 0)


def second_step_kernel(g, place, weighted, gathered, geopot, up, down, late_up, late_down,
                       metric, active, uv0, uv1, uv2, uv3, hh3, qq_own,
                       u_out, v_out, h_out, q1_out, q2_out,
                       qq0, qq1, qq2, qq3, mm, gradient, coriolis, flux0, flux1, uv4, uv5,
                       s_metric, s_inverse, s_active, s_geopot, s_offset,
                       s_uv, s_hh, s_qq, sem):
    n = g.halo
    first = len(FRACTIONS)
    w = g.wide
    s = [time_step * fraction for fraction in FRACTIONS]
    own_copy = pltpu.make_async_copy(qq_own, qq0.at[pl.ds(n, g.rows)], sem.at[0])
    own_copy.start()
    fill_planes(g, up, down, metric, active, s_metric, s_inverse, s_active)
    fill_coriolis(g, coriolis)
    planes = Planes(g, place, s_metric, s_inverse, s_active)
    top = top_half(g)
    for halo, start in ((late_up, 0), (late_down, n + g.rows)):
        for c in range(g.tiles):
            for i in range(n):
                qq0[start + i, :, lane(c)] = halo[i, :, lane(c)]
    me = place[0]
    count = gathered.shape[0]
    height = s_offset.shape[1]
    for c in range(g.tiles):
        s_geopot[c, pl.ds(0, g.margin)] = late_up[n, :, lane(c)]
        s_geopot[c, pl.ds(g.margin, g.rows)] = geopot[:, lane(c)]
        s_geopot[c, pl.ds(g.margin + g.rows, g.margin)] = late_down[n, :, lane(c)]
        offset = jnp.zeros((height, LANES), jnp.float32)
        for other in range(count):
            offset = offset + gathered[other, :, lane(c)] * jnp.where(other > me, 1.0, 0.0)
        s_offset[c] = offset
    geopot_rows = s_geopot.reshape(g.tiles * g.plane, LANES)
    offset_rows = s_offset.reshape(g.tiles * height, LANES)
    shift = g.margin - n

    def one_pair(i, carry):
        e = first + 2 * i
        for c in range(g.tiles):
            base = jnp.where(top, spread(geopot_rows, g.plane, c, e + shift),
                             spread(geopot_rows, g.plane, c, e + 1 + shift))
            offset = jnp.where(top, spread(offset_rows, height, c, 2 * i),
                               spread(offset_rows, height, c, 2 * i + 1))
            one, two = unpack_pair(g, top, base + (weighted[i, :, lane(c)] + offset))
            mm[e, :, lane(c)] = one
            mm[e + 1, :, lane(c)] = two
        return carry

    lax.fori_loop(0, (w - 2 * first) // 2, one_pair, 0)
    fill_gradient(g, first + 1, w - first - 1, mm, gradient)
    fill_flux(g, planes, first, w - first, uv3, hh3, flux0)
    own_copy.wait()
    section(g, planes, 1, w - 1, s[0], uv0, None, tracer=(qq0, qq0, qq1))
    section(g, planes, 2, w - 2, s[1], uv1, None, tracer=(qq1, qq0, qq2))
    section(g, planes, 3, w - 3, s[2], uv2, None, tracer=(qq2, qq0, qq3))
    section(g, planes, 4, w - 4, s[0], uv3, uv3, tracer=(qq3, qq3, qq1),
            mass=(flux0, hh3, gradient, coriolis, uv4, flux1, None))
    section(g, planes, 5, w - 5, s[1], uv4, uv3, tracer=(qq1, qq3, qq2),
            mass=(flux1, hh3, gradient, coriolis, uv5, flux0, None))
    block = g.sub * g.rows

    def store_in(scratch):
        flat = scratch.reshape(g.tiles * block, LANES)

        def store(e, c, value):
            flat[pl.ds(c * block + e - n, g.sub, stride=g.rows), :] = value

        return store

    section(g, planes, 6, w - 6, s[2], uv5, uv3, tracer=(qq2, qq3, store_in(s_qq)),
            mass=(flux0, hh3, gradient, coriolis, store_in(s_uv), None, store_in(s_hh)))
    copies = []
    for target, scratch, slot in ((u_out, s_uv, 0), (v_out, s_uv, 1), (h_out, s_hh, 0),
                                  (q1_out, s_qq, 0), (q2_out, s_qq, 1)):
        for c in range(g.tiles):
            copies.append(pltpu.make_async_copy(
                scratch.at[c, slot], target.at[:, :, lane(c)], sem.at[1]))
    for one in copies:
        one.start()
    for one in copies:
        one.wait()


def local(
    wind_east,
    wind_north,
    thickness,
    tracer_one,
    tracer_two,
    theta_step,
    surface_geopot,
    map_factor,
    active_layers,
):
    layers, rows, columns = thickness.shape
    g = Geometry(layers, rows, columns, layers * lax.axis_size("lev"))
    n, w = g.halo, g.wide
    first = len(FRACTIONS)
    height = -(-(w - 2 * first) // 8) * 8
    count = lax.axis_size("row")
    forward = [(i, (i + 1) % count) for i in range(count)]
    backward = [(i, (i - 1) % count) for i in range(count)]
    place = lax.axis_index("lev").astype(jnp.int32).reshape(1)

    def shape(*dims):
        return jax.ShapeDtypeStruct(dims, jnp.float32)

    def call(body, outs, ins, scratch, name, out_specs=None):
        return pl.pallas_call(
            functools.partial(body, g),
            out_shape=outs,
            in_specs=ins,
            out_specs=out_specs if out_specs is not None else [VMEM] * len(outs),
            scratch_shapes=scratch,
            name=name,
        )

    slab = shape(rows, g.sub, columns)
    broad = shape(w, g.sub, columns)
    fields = pltpu.VMEM((g.tiles, 2, layers, rows, LANES), jnp.float32)
    wide_scratch = pltpu.VMEM((w, g.sub, columns), jnp.float32)
    plane = pltpu.VMEM((g.tiles, g.plane, LANES), jnp.float32)
    offsets = pltpu.VMEM((g.tiles, height, LANES), jnp.float32)
    coriolis = pltpu.VMEM((g.sub, columns), jnp.float32)
    early = n + n // 2 + 2

    up, down, late_up, late_down, uv, hh, qq, mass = call(
        pack_kernel,
        [shape(early, g.sub, columns)] * 2 + [shape(n + 1, g.sub, columns)] * 2
        + [slab] * 3 + [shape(rows, columns)],
        [ANY] * 5 + [VMEM] * 3,
        [fields] * 3 + [pltpu.SemaphoreType.DMA((1,))],
        "pack",
    )(wind_east, wind_north, thickness, tracer_one, tracer_two,
      map_factor, active_layers, surface_geopot)
    up_in = lax.ppermute(up, "row", forward)
    down_in = lax.ppermute(down, "row", backward)
    weighted, below = call(
        exner_kernel, [shape(layers, rows, columns), shape(rows, columns)],
        [SMEM, SMEM, VMEM, VMEM], [], "exner",
    )(place, theta_step, thickness, lax.all_gather(mass, "lev"))
    m_up, m_down, mm = call(
        montgomery_kernel, [shape(n // 2, g.sub, columns)] * 2 + [slab],
        [SMEM, VMEM, VMEM, VMEM], [fields], "montgomery",
    )(place, weighted, lax.all_gather(below, "lev"), surface_geopot)
    m_up_in = lax.ppermute(m_up, "row", forward)
    m_down_in = lax.ppermute(m_down, "row", backward)
    uv0, uv1, uv2, uv3, hh3, mass = call(
        first_step_kernel, [broad] * 5 + [shape(height, columns)],
        [SMEM] + [ANY] * 3 + [VMEM] * 6,
        [wide_scratch] * 5 + [coriolis] + [plane] * 3 + [pltpu.SemaphoreType.DMA((3,))],
        "first_step",
    )(place, uv, hh, mm, up_in, down_in, m_up_in, m_down_in, map_factor, active_layers)
    late_up_in = lax.ppermute(late_up, "row", forward)
    late_down_in = lax.ppermute(late_down, "row", backward)
    weighted, below = call(
        second_exner_kernel,
        [shape((w - 2 * first) // 2, g.sub, columns), shape(height, columns)],
        [SMEM, SMEM, VMEM, VMEM], [offsets], "second_exner",
    )(place, theta_step, hh3, lax.all_gather(mass, "lev"))
    return tuple(call(
        second_step_kernel, [shape(layers, rows, columns)] * 5,
        [SMEM] + [VMEM] * 14 + [ANY],
        [wide_scratch] * 6 + [coriolis] + [wide_scratch] * 4 + [plane] * 4 + [offsets]
        + [fields] * 3 + [pltpu.SemaphoreType.DMA((2,))],
        "second_step", [ANY] * 5,
    )(place, weighted, lax.all_gather(below, "lev"), surface_geopot, up_in, down_in,
      late_up_in, late_down_in, map_factor, active_layers, uv0, uv1, uv2, uv3, hh3, qq))


def solution(mesh):
    state = P("lev", "row", None)
    flat = P("row", None)
    return jax.shard_map(
        local,
        mesh=mesh,
        in_specs=(state,) * 5 + (P(), flat, flat, flat),
        out_specs=(state,) * 5,
        check_vma=False,
    )
```

time: 106 us -> 96.4 us (0.909)
  the two profiles are of different devices: /device:TPU:0 before, /device:TPU:9 now
where the time goes in v1:
time: 96.4 us; the launch traced here: 95.8 us
  Pallas kernels  46.9 us (49%)
  blocking collectives  31.3 us (32%)
  starting transfers between devices  8.07 us (8%)
  waiting for transfers between devices  7.23 us (8%)
  local copies, waits for them, and re-layouts  1.63 us (2%)
    pallas_call x1, Pallas kernels, local(): call(second_step_kernel, [shape(layers, rows, columns)] * 5, [SMEM] + [VM...  19.9 us
    all_gather x2, blocking collectives, local(): lax.all_gather(mass, 'lev')  16.9 us
    pallas_call x1, Pallas kernels, local(): call(first_step_kernel, [broad] * 5 + [shape(height, columns)], [SMEM] +...  15.5 us
    all_gather x2, blocking collectives, local(): lax.all_gather(below, 'lev')  14.4 us
    pallas_call x1, Pallas kernels, local(): call(pack_kernel, [shape(early, g.sub, columns)] * 2 + [shape(n + 1, g.su...  4.82 us
    ppermute x1, waiting for transfers between devices, local(): m_down_in = lax.ppermute(m_down, 'row', backward)  4.41 us
    ppermute x1, starting transfers between devices, local(): late_down_in = lax.ppermute(late_down, 'row', backward)  3.17 us
    ppermute x1, waiting for transfers between devices, local(): m_up_in = lax.ppermute(m_up, 'row', forward)  2.81 us
  transfers between devices with their start and end apart: 6, of which 2 were waited for; matrix products, arithmetic and copies ran while one was open for 0% of the time, Pallas kernels for 23%

profile of v1, /device:TPU:9, one launch (start us, length us, event | category | flops | bytes accessed | tf_op | source)
XLA Modules:
  0.0 95.8 jit_solution(12594376009855689440)
XLA Ops:
  0.6 4.8 %pack.1 = (f32[11,8,1024]{2,1,0:T(8,128)}, f32[11,8,1024]{2,1,0:T(8,128)}, f32[7,8,1024]{2,1,0:T(8,128)}, f32[7,8,1024]{2,1,0:T(8,128)}, f32[16,8,1024]{2,1,0:T(...) custom-call(f32[4,16,1024]{2,1,0:T(8,128)} %u.1, f32[4,16,1024]{2,1,0:T(8,128)} %v.1, ...), custom_call_target="tpu_custom_call" | custom-call | tf_op jit(solution)/shard_map/pack/pallas_call | solution.py:541
  5.5 1.3 %collective-permute-start = (f32[11,8,1024]{2,1,0:T(8,128)}, f32[11,8,1024]{2,1,0:T(8,128)S(1)}, u32[]{:S(2)}, u32[]{:S(2)}) collective-permute-start(f32[11,8,1024]{2,1,0:T(8,128)} %get-tuple-element.32), channel_id=1, source_target_pairs={{0,1},{1,2},{2,3},{3,4},{4,5},{5,6},{6,7},{7,0},{8,9},{9,10},{10,1... | collective-permute-start | bytes 1081352 | tf_op jit(solution)/shard_map/ppermute | solution.py:550
  6.8 1.1 %collective-permute-start.1 = (f32[11,8,1024]{2,1,0:T(8,128)}, f32[11,8,1024]{2,1,0:T(8,128)S(1)}, u32[]{:S(2)}, u32[]{:S(2)}) collective-permute-start(f32[11,8,1024]{2,1,0:T(8,128)} %get-tuple-element.33), channel_id=1, source_target_pairs={{0,7},{1,0},{2,1},{3,2},{4,3},{5,4},{6,5},{7,6},{8,15},{9,8},{10,9... | collective-permute-start | bytes 1081352 | tf_op jit(solution)/shard_map/ppermute | solution.py:551
  7.9 8.4 %all-gather = f32[64,1024]{1,0:T(8,128)} all-gather(f32[16,1024]{1,0:T(8,128)} %get-tuple-element.28), channel_id=2, replica_groups=mesh['lev'=4,'row'=8] {'lev'}, dimensions={0}, use_global_device_ids=true | all-gather | bytes 327680 | tf_op jit(solution)/shard_map/all_gather | solution.py:555
  16.3 1.9 %exner.1 = (f32[4,16,1024]{2,1,0:T(8,128)}, f32[16,1024]{1,0:T(8,128)}) custom-call(s32[1]{0:T(128)} %bitcast.place, f32[16]{0:T(128)} %theta.3, f32[4,16,1024]{2,1,0:T(8,128)} %h.3, f32[4,16,1024]{2,1,0:T(8,128)} %bitcast.7), custom_call_target="tpu_custom_call" | custom-call | tf_op jit(solution)/shard_map/exner/pallas_call | solution.py:552
  18.2 6.8 %all-gather.1 = f32[64,1024]{1,0:T(8,128)} all-gather(f32[16,1024]{1,0:T(8,128)} %get-tuple-element.30), channel_id=3, replica_groups=mesh['lev'=4,'row'=8] {'lev'}, dimensions={0}, use_global_device_ids=true | all-gather | bytes 327680 | tf_op jit(solution)/shard_map/all_gather | solution.py:559
  25.0 0.0 copy-start.7
  25.0 0.0 copy-start.6
  25.0 2.4 %montgomery.1 = (f32[3,8,1024]{2,1,0:T(8,128)}, f32[3,8,1024]{2,1,0:T(8,128)}, f32[16,8,1024]{2,1,0:T(8,128)}) custom-call(s32[1]{0:T(128)} %bitcast.place, f32[4,16,1024]{2,1,0:T(8,128)} %get-tuple-element.29.weighted, f32[4,16,1024]{2,1,0:T(8,128)} %bitcast.8, f32[16,1024]{1,0:T(8,128)} %geopot.5), custom_call_target="tpu_custom_call" | custom-call | tf_op jit(solution)/shard_map/montgomery/pallas_call | solution.py:556
  27.3 0.3 collective-permute-start.2
  27.7 2.0 %collective-permute-start.3 = (f32[3,8,1024]{2,1,0:T(8,128)}, f32[3,8,1024]{2,1,0:T(8,128)S(1)}, u32[]{:S(2)}, u32[]{:S(2)}) collective-permute-start(f32[3,8,1024]{2,1,0:T(8,128)} %get-tuple-element.35), channel_id=1, source_target_pairs={{0,7},{1,0},{2,1},{3,2},{4,3},{5,4},{6,5},{7,6},{8,15},{9,8},{10,9... | collective-permute-start | bytes 294920 | tf_op jit(solution)/shard_map/ppermute | solution.py:561
  29.7 0.0 copy-done.7
  29.7 0.1 collective-permute-start.4
  29.8 2.8 %collective-permute-done.2.m_up = f32[3,8,1024]{2,1,0:T(8,128)S(1)} collective-permute-done((f32[3,8,1024]{2,1,0:T(8,128)}, f32[3,8,1024]{2,1,0:T(8,128)S(1)}, u32[]{:S(2)}, u32[]{:S(2)}) %collective-permute-start.2) | collective-permute-done | bytes 98336 | tf_op jit(solution)/shard_map/ppermute | solution.py:560
  32.6 0.0 copy-start.4
  32.6 0.0 copy-done.6
  32.6 3.2 %collective-permute-start.5 = (f32[7,8,1024]{2,1,0:T(8,128)S(1)}, f32[7,8,1024]{2,1,0:T(8,128)S(1)}, u32[]{:S(2)}, u32[]{:S(2)}) collective-permute-start(f32[7,8,1024]{2,1,0:T(8,128)S(1)} %copy-done.6), channel_id=1, source_target_pairs={{0,7},{1,0},{2,1},{3,2},{4,3},{5,4},{6,5},{7,6},{8,15},{9,8},{10,9... | collective-permute-start | bytes 688136 | tf_op jit(solution)/shard_map/ppermute | solution.py:569
  35.8 4.4 %collective-permute-done.3.m_down = f32[3,8,1024]{2,1,0:T(8,128)S(1)} collective-permute-done((f32[3,8,1024]{2,1,0:T(8,128)}, f32[3,8,1024]{2,1,0:T(8,128)S(1)}, u32[]{:S(2)}, u32[]{:S(2)}) %collective-permute-start.3) | collective-permute-done | bytes 98336 | tf_op jit(solution)/shard_map/ppermute | solution.py:561
  40.2 0.0 copy-start.5
  40.2 0.0 collective-permute-done.up
  40.2 0.0 copy-start
  40.2 0.0 collective-permute-done.1.down
  40.2 0.0 copy-start.1
  40.2 0.0 copy-done.4
  40.3 0.6 copy-done.5
  40.9 0.1 copy-done
  41.0 0.1 copy-done.1
  41.1 15.5 %first_step.1 = (f32[28,8,1024]{2,1,0:T(8,128)}, f32[28,8,1024]{2,1,0:T(8,128)}, f32[28,8,1024]{2,1,0:T(8,128)}, f32[28,8,1024]{2,1,0:T(8,128)}, f32[28,8,1024]{2,1,0:T(8,128)}, /*index=5*/f32[24,1024]{1,0:T(8,128)}) custom-call(s32[1]{0:T(128)} %bitcast.place, f32[16,8,1024]{2,1,0:T(8,128)} %get-tuple-element.26.uv_own, ...), custom_call_target="tpu_custom_call" | custom-call | tf_op jit(solution)/shard_map/first_step/pallas_call | solution.py:562
  56.6 8.5 %all-gather.2 = f32[96,1024]{1,0:T(8,128)} all-gather(f32[24,1024]{1,0:T(8,128)} %get-tuple-element.37), channel_id=4, replica_groups=mesh['lev'=4,'row'=8] {'lev'}, dimensions={0}, use_global_device_ids=true | all-gather | bytes 491520 | tf_op jit(solution)/shard_map/all_gather | solution.py:574
  65.0 2.5 %second_exner.1 = (f32[11,8,1024]{2,1,0:T(8,128)}, f32[24,1024]{1,0:T(8,128)}) custom-call(s32[1]{0:T(128)} %bitcast.place, f32[16]{0:T(128)} %theta.3, f32[28,8,1024]{2,1,0:T(8,128)} %get-tuple-element.36.hh.hh3, f32[4,24,1024]{2,1,0:T(8,128)} %bitcast.6), custom_call_target="tpu_custom_call" | custom-call | tf_op jit(solution)/shard_map/second_exner/pallas_call | solution.py:570
  67.6 7.6 %all-gather.3 = f32[96,1024]{1,0:T(8,128)} all-gather(f32[24,1024]{1,0:T(8,128)} %get-tuple-element.39), channel_id=5, replica_groups=mesh['lev'=4,'row'=8] {'lev'}, dimensions={0}, use_global_device_ids=true | all-gather | bytes 491520 | tf_op jit(solution)/shard_map/all_gather | solution.py:581
  75.2 0.0 collective-permute-done.4.late_up
  75.2 0.0 copy-start.2
  75.2 0.0 collective-permute-done.5.late_down
  75.2 0.0 copy-start.3
  75.2 0.7 copy-done.2
  75.8 0.1 copy-done.3
  76.0 19.9 %second_step.1 = (f32[4,16,1024]{2,1,0:T(8,128)}, f32[4,16,1024]{2,1,0:T(8,128)}, f32[4,16,1024]{2,1,0:T(8,128)}, f32[4,16,1024]{2,1,0:T(8,128)}, f32[4,16,1024]{2,1,0:T(8,128)}) custom-call(s32[1]{0:T(128)} %bitcast.place, f32[11,8,1024]{2,1,0:T(8,128)} %get-tuple-element.38.weighted, f32[4,24,1024]{2,1,0:T(8,128)} %bitcast.5, f32[16,1024]{1,0:T(8,128)} %geopot.5, ...), custom_call_target="tpu_custom_call" | custom-call | tf_op jit(solution)/shard_map/second_step/pallas_call | solution.py:575
Async XLA Ops:
  5.5 34.8 %collective-permute-start = (f32[11,8,1024]{2,1,0:T(8,128)}, f32[11,8,1024]{2,1,0:T(8,128)S(1)}, u32[]{:S(2)}, u32[]{:S(2)}) collective-permute-start(f32[11,8,1024]{2,1,0:T(8,128)} %get-tuple-element.32), channel_id=1, source_target_pairs={{0,1},{1,2},{2,3},{3,4},{4,5},{5,6},{6,7},{7,0},{8,9},{9,10},{10,1... | collective-permute-start | bytes 1081352 | tf_op jit(solution)/shard_map/ppermute | solution.py:550
  6.8 33.5 %collective-permute-start.1 = (f32[11,8,1024]{2,1,0:T(8,128)}, f32[11,8,1024]{2,1,0:T(8,128)S(1)}, u32[]{:S(2)}, u32[]{:S(2)}) collective-permute-start(f32[11,8,1024]{2,1,0:T(8,128)} %get-tuple-element.33), channel_id=1, source_target_pairs={{0,7},{1,0},{2,1},{3,2},{4,3},{5,4},{6,5},{7,6},{8,15},{9,8},{10,9... | collective-permute-start | bytes 1081352 | tf_op jit(solution)/shard_map/ppermute | solution.py:551
  25.0 4.7 %copy-start.7 = (f32[7,8,1024]{2,1,0:T(8,128)S(1)}, f32[7,8,1024]{2,1,0:T(8,128)}, u32[]{:S(2)}) copy-start(f32[7,8,1024]{2,1,0:T(8,128)} %get-tuple-element.40) | copy-start | bytes 688132
  25.0 7.7 %copy-start.6 = (f32[7,8,1024]{2,1,0:T(8,128)S(1)}, f32[7,8,1024]{2,1,0:T(8,128)}, u32[]{:S(2)}) copy-start(f32[7,8,1024]{2,1,0:T(8,128)} %get-tuple-element.41) | copy-start | bytes 688132
  27.3 5.3 %collective-permute-start.2 = (f32[3,8,1024]{2,1,0:T(8,128)}, f32[3,8,1024]{2,1,0:T(8,128)S(1)}, u32[]{:S(2)}, u32[]{:S(2)}) collective-permute-start(f32[3,8,1024]{2,1,0:T(8,128)} %get-tuple-element.34), channel_id=1, source_target_pairs={{0,1},{1,2},{2,3},{3,4},{4,5},{5,6},{6,7},{7,0},{8,9},{9,10},{10,1... | collective-permute-start | bytes 294920 | tf_op jit(solution)/shard_map/ppermute | solution.py:560
  27.7 12.5 %collective-permute-start.3 = (f32[3,8,1024]{2,1,0:T(8,128)}, f32[3,8,1024]{2,1,0:T(8,128)S(1)}, u32[]{:S(2)}, u32[]{:S(2)}) collective-permute-start(f32[3,8,1024]{2,1,0:T(8,128)} %get-tuple-element.35), channel_id=1, source_target_pairs={{0,7},{1,0},{2,1},{3,2},{4,3},{5,4},{6,5},{7,6},{8,15},{9,8},{10,9... | collective-permute-start | bytes 294920 | tf_op jit(solution)/shard_map/ppermute | solution.py:561
  29.7 45.5 %collective-permute-start.4 = (f32[7,8,1024]{2,1,0:T(8,128)S(1)}, f32[7,8,1024]{2,1,0:T(8,128)S(1)}, u32[]{:S(2)}, u32[]{:S(2)}) collective-permute-start(f32[7,8,1024]{2,1,0:T(8,128)S(1)} %copy-done.7), channel_id=1, source_target_pairs={{0,1},{1,2},{2,3},{3,4},{4,5},{5,6},{6,7},{7,0},{8,9},{9,10},{10,1... | collective-permute-start | bytes 688136 | tf_op jit(solution)/shard_map/ppermute | solution.py:568
  32.6 7.6 %copy-start.4 = (f32[3,8,1024]{2,1,0:T(8,128)}, f32[3,8,1024]{2,1,0:T(8,128)S(1)}, u32[]{:S(2)}) copy-start(f32[3,8,1024]{2,1,0:T(8,128)S(1)} %collective-permute-done.2.m_up) | copy-start | bytes 294916
  32.6 42.5 %collective-permute-start.5 = (f32[7,8,1024]{2,1,0:T(8,128)S(1)}, f32[7,8,1024]{2,1,0:T(8,128)S(1)}, u32[]{:S(2)}, u32[]{:S(2)}) collective-permute-start(f32[7,8,1024]{2,1,0:T(8,128)S(1)} %copy-done.6), channel_id=1, source_target_pairs={{0,7},{1,0},{2,1},{3,2},{4,3},{5,4},{6,5},{7,6},{8,15},{9,8},{10,9... | collective-permute-start | bytes 688136 | tf_op jit(solution)/shard_map/ppermute | solution.py:569
  40.2 0.6 copy-start.5
  40.2 0.8 copy-start
  40.2 0.9 copy-start.1
  75.2 0.7 copy-start.2
  75.2 0.8 copy-start.3

commit v2 on v1

--- a/solution.py
+++ b/solution.py
@@ -10,6 +10,7 @@
 OUTER = 2
 FRACTIONS = (1.0 / 3.0, 0.5, 1.0)
 LANES = 128
+SCOPED_BYTES = 24 * 1024 * 1024
 
 time_step = 0.05
 top_pressure = 0.1
@@ -517,7 +518,10 @@
     place = lax.axis_index("lev").astype(jnp.int32).reshape(1)
 
     def shape(*dims):
-        return jax.ShapeDtypeStruct(dims, jnp.float32)
+        return pltpu.VMEM(dims, jnp.float32)
+
+    def near(value):
+        return pltpu.with_memory_space_constraint(value, pltpu.VMEM)
 
     def call(body, outs, ins, scratch, name, out_specs=None):
         return pl.pallas_call(
@@ -526,6 +530,7 @@
             in_specs=ins,
             out_specs=out_specs if out_specs is not None else [VMEM] * len(outs),
             scratch_shapes=scratch,
+            compiler_params=pltpu.CompilerParams(vmem_limit_bytes=SCOPED_BYTES),
             name=name,
         )
 
@@ -547,38 +552,38 @@
         "pack",
     )(wind_east, wind_north, thickness, tracer_one, tracer_two,
       map_factor, active_layers, surface_geopot)
-    up_in = lax.ppermute(up, "row", forward)
-    down_in = lax.ppermute(down, "row", backward)
+    up_in = near(lax.ppermute(up, "row", forward))
+    down_in = near(lax.ppermute(down, "row", backward))
     weighted, below = call(
         exner_kernel, [shape(layers, rows, columns), shape(rows, columns)],
         [SMEM, SMEM, VMEM, VMEM], [], "exner",
-    )(place, theta_step, thickness, lax.all_gather(mass, "lev"))
+    )(place, theta_step, thickness, near(lax.all_gather(mass, "lev")))
     m_up, m_down, mm = call(
         montgomery_kernel, [shape(n // 2, g.sub, columns)] * 2 + [slab],
         [SMEM, VMEM, VMEM, VMEM], [fields], "montgomery",
-    )(place, weighted, lax.all_gather(below, "lev"), surface_geopot)
-    m_up_in = lax.ppermute(m_up, "row", forward)
-    m_down_in = lax.ppermute(m_down, "row", backward)
+    )(place, weighted, near(lax.all_gather(below, "lev")), surface_geopot)
+    m_up_in = near(lax.ppermute(m_up, "row", forward))
+    m_down_in = near(lax.ppermute(m_down, "row", backward))
     uv0, uv1, uv2, uv3, hh3, mass = call(
         first_step_kernel, [broad] * 5 + [shape(height, columns)],
         [SMEM] + [ANY] * 3 + [VMEM] * 6,
         [wide_scratch] * 5 + [coriolis] + [plane] * 3 + [pltpu.SemaphoreType.DMA((3,))],
         "first_step",
     )(place, uv, hh, mm, up_in, down_in, m_up_in, m_down_in, map_factor, active_layers)
-    late_up_in = lax.ppermute(late_up, "row", forward)
-    late_down_in = lax.ppermute(late_down, "row", backward)
+    late_up_in = near(lax.ppermute(late_up, "row", forward))
+    late_down_in = near(lax.ppermute(late_down, "row", backward))
     weighted, below = call(
         second_exner_kernel,
         [shape((w - 2 * first) // 2, g.sub, columns), shape(height, columns)],
         [SMEM, SMEM, VMEM, VMEM], [offsets], "second_exner",
-    )(place, theta_step, hh3, lax.all_gather(mass, "lev"))
+    )(place, theta_step, hh3, near(lax.all_gather(mass, "lev")))
     return tuple(call(
-        second_step_kernel, [shape(layers, rows, columns)] * 5,
+        second_step_kernel, [jax.ShapeDtypeStruct((layers, rows, columns), jnp.float32)] * 5,
         [SMEM] + [VMEM] * 14 + [ANY],
         [wide_scratch] * 6 + [coriolis] + [wide_scratch] * 4 + [plane] * 4 + [offsets]
         + [fields] * 3 + [pltpu.SemaphoreType.DMA((2,))],
         "second_step", [ANY] * 5,
-    )(place, weighted, lax.all_gather(below, "lev"), surface_geopot, up_in, down_in,
+    )(place, weighted, near(lax.all_gather(below, "lev")), surface_geopot, up_in, down_in,
       late_up_in, late_down_in, map_factor, active_layers, uv0, uv1, uv2, uv3, hh3, qq))
 
 

time: 96.4 us -> 83.5 us (0.87)
  the two profiles are of different devices: /device:TPU:9 before, /device:TPU:0 now
where the time goes in v2:
time: 83.5 us; the launch traced here: 82.2 us
  Pallas kernels  31.7 us (38%)
  blocking collectives  24.9 us (30%)
  starting transfers between devices  12.5 us (15%)
  local copies, waits for them, and re-layouts  9.31 us (11%)
  waiting for transfers between devices  3.03 us (4%)
    pallas_call x1, Pallas kernels, local(): call(second_step_kernel, [jax.ShapeDtypeStruct((layers, rows, columns), j...  17 us
    all_gather x2, blocking collectives, local(): lax.all_gather(below, 'lev')  12.6 us
    all_gather x2, blocking collectives, local(): lax.all_gather(mass, 'lev')  12.4 us
    pallas_call x1, Pallas kernels, local(): call(first_step_kernel, [broad] * 5 + [shape(height, columns)], [SMEM] +...  11.2 us
    unnamed x34, local copies, waits for them, and re-layouts  9.31 us
    ppermute x1, starting transfers between devices, local(): m_down_in = near(lax.ppermute(m_down, 'row', backward))  4.71 us
    ppermute x1, starting transfers between devices, local(): down_in = near(lax.ppermute(down, 'row', backward))  3.04 us
    ppermute x1, waiting for transfers between devices, local(): m_up_in = near(lax.ppermute(m_up, 'row', forward))  3.02 us
  transfers between devices with their start and end apart: 6, of which 1 were waited for; matrix products, arithmetic and copies ran while one was open for 0% of the time, Pallas kernels for 16%

profile of v2, /device:TPU:0, one launch (start us, length us, event | category | flops | bytes accessed | tf_op | source)
XLA Modules:
  0.0 82.2 jit_solution(3936924474638693344)
XLA Ops:
  0.6 0.0 copy-start
  0.6 0.9 %copy-done = f32[4,16,1024]{2,1,0:T(8,128)S(1)} copy-done((f32[4,16,1024]{2,1,0:T(8,128)S(1)}, f32[4,16,1024]{2,1,0:T(8,128)}, u32[]{:S(2)}) %copy-start) | copy-done | bytes 262168
  1.6 0.0 copy-start.2
  1.6 0.8 %copy-done.2 = f32[16,1024]{1,0:T(8,128)S(1)} copy-done((f32[16,1024]{1,0:T(8,128)S(1)}, f32[16,1024]{1,0:T(8,128)}, u32[]{:S(2)}) %copy-start.2) | copy-done | bytes 65560
  2.4 0.0 copy-start.4
  2.4 0.8 %copy-done.4 = s32[16,1024]{1,0:T(8,128)S(1)} copy-done((s32[16,1024]{1,0:T(8,128)S(1)}, s32[16,1024]{1,0:T(8,128)}, u32[]{:S(2)}) %copy-start.4) | copy-done | bytes 65560
  3.3 0.0 copy-start.6
  3.3 0.8 %copy-done.6 = f32[16,1024]{1,0:T(8,128)S(1)} copy-done((f32[16,1024]{1,0:T(8,128)S(1)}, f32[16,1024]{1,0:T(8,128)}, u32[]{:S(2)}) %copy-start.6) | copy-done | bytes 65560
  4.1 0.0 copy-start.8
  4.1 0.9 %copy-done.8 = f32[4,16,1024]{2,1,0:T(8,128)S(1)} copy-done((f32[4,16,1024]{2,1,0:T(8,128)S(1)}, f32[4,16,1024]{2,1,0:T(8,128)}, u32[]{:S(2)}) %copy-start.8) | copy-done | bytes 262168
  5.1 0.0 copy-start.9
  5.1 0.9 %copy-done.9 = f32[4,16,1024]{2,1,0:T(8,128)S(1)} copy-done((f32[4,16,1024]{2,1,0:T(8,128)S(1)}, f32[4,16,1024]{2,1,0:T(8,128)}, u32[]{:S(2)}) %copy-start.9) | copy-done | bytes 262168
  6.0 0.9 %copy-done.10 = f32[4,16,1024]{2,1,0:T(8,128)S(1)} copy-done((f32[4,16,1024]{2,1,0:T(8,128)S(1)}, f32[4,16,1024]{2,1,0:T(8,128)}, u32[]{:S(2)}) %copy-start.10) | copy-done | bytes 262168
  7.0 0.9 %copy-done.11 = f32[4,16,1024]{2,1,0:T(8,128)S(1)} copy-done((f32[4,16,1024]{2,1,0:T(8,128)S(1)}, f32[4,16,1024]{2,1,0:T(8,128)}, u32[]{:S(2)}) %copy-start.11) | copy-done | bytes 262168
  7.9 1.4 %pack.1 = (f32[11,8,1024]{2,1,0:T(8,128)S(1)}, f32[11,8,1024]{2,1,0:T(8,128)S(1)}, f32[7,8,1024]{2,1,0:T(8,128)S(1)}, f32[7,8,1024]{2,1,0:T(8,128)S(1)}, f32[16,...) custom-call(f32[4,16,1024]{2,1,0:T(8,128)S(1)} %copy-done.8, ...), custom_call_target="tpu_custom_call" | custom-call | tf_op jit(solution)/shard_map/pack/pallas_call | solution.py:546
  9.3 0.0 copy-start.13
  9.3 0.7 copy-done.13
  10.0 0.7 copy-done.15
  10.7 3.0 %collective-permute-start = (f32[11,8,1024]{2,1,0:T(8,128)S(1)}, f32[11,8,1024]{2,1,0:T(8,128)S(1)}, u32[]{:S(2)}, u32[]{:S(2)}) collective-permute-start(f32[11,8,1024]{2,1,0:T(8,128)S(1)} %get-tuple-element.32), channel_id=1, source_target_pairs={{0,1},{1,2},{2,3},{3,4},{4,5},{5,6},{6,7},{7,0},{8,9},{9,10},{10,1... | collective-permute-start | bytes 1081352 | tf_op jit(solution)/shard_map/ppermute | solution.py:555
  13.7 3.0 %collective-permute-start.1 = (f32[11,8,1024]{2,1,0:T(8,128)S(1)}, f32[11,8,1024]{2,1,0:T(8,128)S(1)}, u32[]{:S(2)}, u32[]{:S(2)}) collective-permute-start(f32[11,8,1024]{2,1,0:T(8,128)S(1)} %get-tuple-element.33), channel_id=1, source_target_pairs={{0,7},{1,0},{2,1},{3,2},{4,3},{5,4},{6,5},{7,6},{8,15},{9,8},{10,9... | collective-permute-start | bytes 1081352 | tf_op jit(solution)/shard_map/ppermute | solution.py:556
  16.7 5.9 %all-gather = f32[64,1024]{1,0:T(8,128)S(1)} all-gather(f32[16,1024]{1,0:T(8,128)S(1)} %get-tuple-element.28), channel_id=2, replica_groups=mesh['lev'=4,'row'=8] {'lev'}, dimensions={0}, use_global_device_ids=true | all-gather | bytes 327680 | tf_op jit(solution)/shard_map/all_gather | solution.py:560
  22.6 0.0 copy-done.1
  22.6 0.7 copy-done.12
  23.3 0.7 exner.1
  24.0 0.0 copy-start.7
  24.0 6.0 %all-gather.1 = f32[64,1024]{1,0:T(8,128)S(1)} all-gather(f32[16,1024]{1,0:T(8,128)S(1)} %get-tuple-element.30), channel_id=3, replica_groups=mesh['lev'=4,'row'=8] {'lev'}, dimensions={0}, use_global_device_ids=true | all-gather | bytes 327680 | tf_op jit(solution)/shard_map/all_gather | solution.py:564
  30.0 0.0 copy-done.7
  30.0 0.0 copy-start.5
  30.0 0.4 montgomery.1
  30.4 0.1 collective-permute-start.2
  30.5 4.7 %collective-permute-start.3 = (f32[3,8,1024]{2,1,0:T(8,128)S(1)}, f32[3,8,1024]{2,1,0:T(8,128)S(1)}, u32[]{:S(2)}, u32[]{:S(2)}) collective-permute-start(f32[3,8,1024]{2,1,0:T(8,128)S(1)} %get-tuple-element.35), channel_id=1, source_target_pairs={{0,7},{1,0},{2,1},{3,2},{4,3},{5,4},{6,5},{7,6},{8,15},{9,8},{10,9... | collective-permute-start | bytes 294920 | tf_op jit(solution)/shard_map/ppermute | solution.py:566
  35.2 0.0 copy-done.16
  35.2 0.0 collective-permute-start.4
  35.2 3.0 %collective-permute-done.2.m_up = f32[3,8,1024]{2,1,0:T(8,128)S(1)} collective-permute-done((f32[3,8,1024]{2,1,0:T(8,128)S(1)}, f32[3,8,1024]{2,1,0:T(8,128)S(1)}, u32[]{:S(2)}, u32[]{:S(2)}) %collective-permute-start.2) | collective-permute-done | bytes 98336 | tf_op jit(solution)/shard_map/ppermute | solution.py:565
  38.2 0.0 copy-done.14
  38.2 1.7 %collective-permute-start.5 = (f32[7,8,1024]{2,1,0:T(8,128)S(1)}, f32[7,8,1024]{2,1,0:T(8,128)S(1)}, u32[]{:S(2)}, u32[]{:S(2)}) collective-permute-start(f32[7,8,1024]{2,1,0:T(8,128)S(1)} %copy-done.14), channel_id=1, source_target_pairs={{0,7},{1,0},{2,1},{3,2},{4,3},{5,4},{6,5},{7,6},{8,15},{9,8},{10,9... | collective-permute-start | bytes 688136 | tf_op jit(solution)/shard_map/ppermute | solution.py:574
  39.9 0.0 collective-permute-done.3.m_down
  39.9 0.0 collective-permute-done.up
  40.0 0.0 collective-permute-done.1.down
  40.0 0.0 copy-done.3
  40.0 0.0 copy-done.5
  40.0 11.2 %first_step.1 = (f32[28,8,1024]{2,1,0:T(8,128)S(1)}, f32[28,8,1024]{2,1,0:T(8,128)S(1)}, f32[28,8,1024]{2,1,0:T(8,128)S(1)}, f32[28,8,1024]{2,1,0:T(8,128)S(1)},...) custom-call(s32[1]{0:T(128)} %bitcast.place, f32[16,8,1024]{2,1,0:T(8,128)S(1)} %get-tuple-element.26.uv_own, ...), custom_call_target="tpu_custom_call" | custom-call | tf_op jit(solution)/shard_map/first_step/pallas_call | solution.py:567
  51.2 6.5 %all-gather.2 = f32[96,1024]{1,0:T(8,128)S(1)} all-gather(f32[24,1024]{1,0:T(8,128)S(1)} %get-tuple-element.37), channel_id=4, replica_groups=mesh['lev'=4,'row'=8] {'lev'}, dimensions={0}, use_global_device_ids=true | all-gather | bytes 491520 | tf_op jit(solution)/shard_map/all_gather | solution.py:579
  57.7 1.0 %second_exner.1 = (f32[11,8,1024]{2,1,0:T(8,128)S(1)}, f32[24,1024]{1,0:T(8,128)S(1)}) custom-call(s32[1]{0:T(128)} %bitcast.place, f32[16]{0:T(128)S(1)} %copy-done.12, f32[28,8,1024]{2,1,0:T(8,128)S(1)} %get-tuple-element.36.hh.hh3, f32[4,24,1024]{2,1,0:T(8,128)S(1)} %bitcast.6), custom_call_target="tpu_custom_call" | custom-call | tf_op jit(solution)/shard_map/second_exner/pallas_call | solution.py:575
  58.7 6.6 %all-gather.3 = f32[96,1024]{1,0:T(8,128)S(1)} all-gather(f32[24,1024]{1,0:T(8,128)S(1)} %get-tuple-element.39), channel_id=5, replica_groups=mesh['lev'=4,'row'=8] {'lev'}, dimensions={0}, use_global_device_ids=true | all-gather | bytes 491520 | tf_op jit(solution)/shard_map/all_gather | solution.py:586
  65.3 0.0 collective-permute-done.4.late_up
  65.3 0.0 collective-permute-done.5.late_down
  65.3 17.0 %second_step.1 = (f32[4,16,1024]{2,1,0:T(8,128)}, f32[4,16,1024]{2,1,0:T(8,128)}, f32[4,16,1024]{2,1,0:T(8,128)}, f32[4,16,1024]{2,1,0:T(8,128)}, f32[4,16,1024]{2,1,0:T(8,128)}) custom-call(s32[1]{0:T(128)} %bitcast.place, f32[11,8,1024]{2,1,0:T(8,128)S(1)} %get-tuple-element.38.weighted, f32[4,24,1024]{2,1,0:T(8,128)S(1)} %bitcast.5, ...), custom_call_target="tpu_custom_call" | custom-call | tf_op jit(solution)/shard_map/second_step/pallas_call | solution.py:580
  (8 shorter events, 0.0 us)
Async XLA Ops:
  0.6 1.0 %copy-start = (f32[4,16,1024]{2,1,0:T(8,128)S(1)}, f32[4,16,1024]{2,1,0:T(8,128)}, u32[]{:S(2)}) copy-start(f32[4,16,1024]{2,1,0:T(8,128)} %h.3) | copy-start | bytes 786436
  1.6 0.8 %copy-start.2 = (f32[16,1024]{1,0:T(8,128)S(1)}, f32[16,1024]{1,0:T(8,128)}, u32[]{:S(2)}) copy-start(f32[16,1024]{1,0:T(8,128)} %metric.5) | copy-start | bytes 196612
  2.4 0.8 %copy-start.4 = (s32[16,1024]{1,0:T(8,128)S(1)}, s32[16,1024]{1,0:T(8,128)}, u32[]{:S(2)}) copy-start(s32[16,1024]{1,0:T(8,128)} %active.5) | copy-start | bytes 196612
  3.3 0.8 %copy-start.6 = (f32[16,1024]{1,0:T(8,128)S(1)}, f32[16,1024]{1,0:T(8,128)}, u32[]{:S(2)}) copy-start(f32[16,1024]{1,0:T(8,128)} %geopot.5) | copy-start | bytes 196612
  4.1 0.9 %copy-start.8 = (f32[4,16,1024]{2,1,0:T(8,128)S(1)}, f32[4,16,1024]{2,1,0:T(8,128)}, u32[]{:S(2)}) copy-start(f32[4,16,1024]{2,1,0:T(8,128)} %u.1) | copy-start | bytes 786436
  5.1 0.9 %copy-start.9 = (f32[4,16,1024]{2,1,0:T(8,128)S(1)}, f32[4,16,1024]{2,1,0:T(8,128)}, u32[]{:S(2)}) copy-start(f32[4,16,1024]{2,1,0:T(8,128)} %v.1) | copy-start | bytes 786436
  6.0 0.9 %copy-start.10 = (f32[4,16,1024]{2,1,0:T(8,128)S(1)}, f32[4,16,1024]{2,1,0:T(8,128)}, u32[]{:S(2)}) copy-start(f32[4,16,1024]{2,1,0:T(8,128)} %q1.1) | copy-start | bytes 786436
  7.0 0.9 %copy-start.11 = (f32[4,16,1024]{2,1,0:T(8,128)S(1)}, f32[4,16,1024]{2,1,0:T(8,128)}, u32[]{:S(2)}) copy-start(f32[4,16,1024]{2,1,0:T(8,128)} %q2.1) | copy-start | bytes 786436
  9.3 0.7 copy-start.13
  10.0 0.7 copy-start.15
  10.7 11.9 %copy-start.1 = (f32[4,16,1024]{2,1,0:T(8,128)S(1)}, f32[4,16,1024]{2,1,0:T(8,128)}, u32[]{:S(2)}) copy-start(f32[4,16,1024]{2,1,0:T(8,128)} %h.3) | copy-start | bytes 786436
  10.7 29.2 %collective-permute-start = (f32[11,8,1024]{2,1,0:T(8,128)S(1)}, f32[11,8,1024]{2,1,0:T(8,128)S(1)}, u32[]{:S(2)}, u32[]{:S(2)}) collective-permute-start(f32[11,8,1024]{2,1,0:T(8,128)S(1)} %get-tuple-element.32), channel_id=1, source_target_pairs={{0,1},{1,2},{2,3},{3,4},{4,5},{5,6},{6,7},{7,0},{8,9},{9,10},{10,1... | collective-permute-start | bytes 1081352 | tf_op jit(solution)/shard_map/ppermute | solution.py:555
  13.7 26.2 %collective-permute-start.1 = (f32[11,8,1024]{2,1,0:T(8,128)S(1)}, f32[11,8,1024]{2,1,0:T(8,128)S(1)}, u32[]{:S(2)}, u32[]{:S(2)}) collective-permute-start(f32[11,8,1024]{2,1,0:T(8,128)S(1)} %get-tuple-element.33), channel_id=1, source_target_pairs={{0,7},{1,0},{2,1},{3,2},{4,3},{5,4},{6,5},{7,6},{8,15},{9,8},{10,9... | collective-permute-start | bytes 1081352 | tf_op jit(solution)/shard_map/ppermute | solution.py:556
  22.6 0.7 copy-start.12
  24.0 6.0 %copy-start.7 = (f32[16,1024]{1,0:T(8,128)S(1)}, f32[16,1024]{1,0:T(8,128)}, u32[]{:S(2)}) copy-start(f32[16,1024]{1,0:T(8,128)} %geopot.5) | copy-start | bytes 196612
  30.0 5.2 %copy-start.16 = (f32[7,8,1024]{2,1,0:T(8,128)S(1)}, f32[7,8,1024]{2,1,0:T(8,128)}, u32[]{:S(2)}) copy-start(f32[7,8,1024]{2,1,0:T(8,128)} %copy-done.15) | copy-start | bytes 688132
  30.0 8.3 %copy-start.14 = (f32[7,8,1024]{2,1,0:T(8,128)S(1)}, f32[7,8,1024]{2,1,0:T(8,128)}, u32[]{:S(2)}) copy-start(f32[7,8,1024]{2,1,0:T(8,128)} %copy-done.13) | copy-start | bytes 688132
  30.0 10.0 %copy-start.3 = (f32[16,1024]{1,0:T(8,128)S(1)}, f32[16,1024]{1,0:T(8,128)}, u32[]{:S(2)}) copy-start(f32[16,1024]{1,0:T(8,128)} %metric.5) | copy-start | bytes 196612
  30.0 10.0 %copy-start.5 = (s32[16,1024]{1,0:T(8,128)S(1)}, s32[16,1024]{1,0:T(8,128)}, u32[]{:S(2)}) copy-start(s32[16,1024]{1,0:T(8,128)} %active.5) | copy-start | bytes 196612
  30.4 7.8 %collective-permute-start.2 = (f32[3,8,1024]{2,1,0:T(8,128)S(1)}, f32[3,8,1024]{2,1,0:T(8,128)S(1)}, u32[]{:S(2)}, u32[]{:S(2)}) collective-permute-start(f32[3,8,1024]{2,1,0:T(8,128)S(1)} %get-tuple-element.34), channel_id=1, source_target_pairs={{0,1},{1,2},{2,3},{3,4},{4,5},{5,6},{6,7},{7,0},{8,9},{9,10},{10,1... | collective-permute-start | bytes 294920 | tf_op jit(solution)/shard_map/ppermute | solution.py:565
  30.5 9.4 %collective-permute-start.3 = (f32[3,8,1024]{2,1,0:T(8,128)S(1)}, f32[3,8,1024]{2,1,0:T(8,128)S(1)}, u32[]{:S(2)}, u32[]{:S(2)}) collective-permute-start(f32[3,8,1024]{2,1,0:T(8,128)S(1)} %get-tuple-element.35), channel_id=1, source_target_pairs={{0,7},{1,0},{2,1},{3,2},{4,3},{5,4},{6,5},{7,6},{8,15},{9,8},{10,9... | collective-permute-start | bytes 294920 | tf_op jit(solution)/shard_map/ppermute | solution.py:566
  35.2 30.1 %collective-permute-start.4 = (f32[7,8,1024]{2,1,0:T(8,128)S(1)}, f32[7,8,1024]{2,1,0:T(8,128)S(1)}, u32[]{:S(2)}, u32[]{:S(2)}) collective-permute-start(f32[7,8,1024]{2,1,0:T(8,128)S(1)} %copy-done.16), channel_id=1, source_target_pairs={{0,1},{1,2},{2,3},{3,4},{4,5},{5,6},{6,7},{7,0},{8,9},{9,10},{10,1... | collective-permute-start | bytes 688136 | tf_op jit(solution)/shard_map/ppermute | solution.py:573
  38.2 27.0 %collective-permute-start.5 = (f32[7,8,1024]{2,1,0:T(8,128)S(1)}, f32[7,8,1024]{2,1,0:T(8,128)S(1)}, u32[]{:S(2)}, u32[]{:S(2)}) collective-permute-start(f32[7,8,1024]{2,1,0:T(8,128)S(1)} %copy-done.14), channel_id=1, source_target_pairs={{0,7},{1,0},{2,1},{3,2},{4,3},{5,4},{6,5},{7,6},{8,15},{9,8},{10,9... | collective-permute-start | bytes 688136 | tf_op jit(solution)/shard_map/ppermute | solution.py:574

commit v3 on v2

v3 whole, which is shorter than its diff:
```python
import functools

import jax
import jax.numpy as jnp
from jax import lax
from jax.experimental import pallas as pl
from jax.experimental.pallas import tpu as pltpu
from jax.sharding import PartitionSpec as P

OUTER = 2
FRACTIONS = (1.0 / 3.0, 0.5, 1.0)
LANES = 128
SCOPED_BYTES = 16 * 1024 * 1024

time_step = 0.05
top_pressure = 0.1
exner_power = 2.0 / 7.0

VMEM = pl.BlockSpec(memory_space=pltpu.VMEM)
SMEM = pl.BlockSpec(memory_space=pltpu.SMEM)
FAR = pl.BlockSpec(memory_space=pltpu.HBM)


class Geometry:
    def __init__(self, layers, rows, columns, levels):
        self.layers, self.rows, self.columns, self.levels = layers, rows, columns, levels
        self.sub = 2 * layers
        self.tiles = columns // LANES
        self.halo = OUTER * len(FRACTIONS)
        self.wide = rows + 2 * self.halo
        self.margin = 8
        self.plane = rows + 2 * self.margin
        assert self.sub == 8 and columns % LANES == 0 and rows % 8 == 0
        assert self.halo % 2 == 0 and self.halo <= self.margin <= rows


def lane(c):
    return pl.ds(c * LANES, LANES)


def sublane_index(g):
    return lax.broadcasted_iota(jnp.int32, (g.sub, LANES), 0)


def top_half(g):
    return sublane_index(g) < g.layers


def swap_halves(g, value):
    return pltpu.roll(value, g.layers, 0)


def column_differences(g, values, edge):
    lanes = lax.broadcasted_iota(jnp.int32, (g.sub, LANES), 1)
    first, last = lanes == 0, lanes == LANES - 1
    right_moved = [pltpu.roll(v, 1, 1) for v in values]
    left_moved = [pltpu.roll(v, LANES - 1, 1) for v in values]
    zero = jnp.zeros((g.sub, LANES), jnp.float32)
    result = []
    for c in range(g.tiles):
        before = right_moved[c - 1] if c > 0 else (values[c] if edge else zero)
        after = left_moved[c + 1] if c < g.tiles - 1 else (values[c] if edge else zero)
        result.append(
            jnp.where(last, after, left_moved[c]) - jnp.where(first, before, right_moved[c])
        )
    return result


def row_of(g, ref, e):
    return [ref[e, :, lane(c)] for c in range(g.tiles)]


def spread(flat, height, c, row):
    return flat[pl.ds(c * height + row, 8, stride=0), :]


def copy_fields(g, fields, scratch, sem):
    copies = []
    for slot, field in enumerate(fields):
        for c in range(g.tiles):
            copies.append(
                pltpu.make_async_copy(field.at[:, :, lane(c)], scratch.at[c, slot], sem)
            )
    return copies


def pack_kernel(g, u, v, h, q1, q2, metric, active, geopot, theta,
                up, down, late_up, late_down, uv, hh, qq, mass, own_metric, own_active, jumps,
                s_uv, s_hh, s_qq, s_active, s_geopot, s_theta, sem):
    copies = (copy_fields(g, (h, h), s_hh, sem.at[0]) + copy_fields(g, (u, v), s_uv, sem.at[0])
              + [pltpu.make_async_copy(metric, own_metric, sem.at[0]),
                 pltpu.make_async_copy(active, s_active, sem.at[0])])
    others = copy_fields(g, (q1, q2), s_qq, sem.at[1]) + [
        pltpu.make_async_copy(geopot, s_geopot, sem.at[1]),
        pltpu.make_async_copy(theta, s_theta, sem.at[2])]
    for one in copies + others:
        one.start()
    for one in copies:
        one.wait()
    for c in range(g.tiles):
        total = jnp.abs(s_hh[c, 0, 0])
        for k in range(1, g.layers):
            total = total + jnp.abs(s_hh[c, 0, k])
        mass[:, lane(c)] = total
        own_active[:, lane(c)] = s_active[:, lane(c)].astype(jnp.float32)
    block = g.sub * g.rows

    def gather_rows(source, target):
        flat = source.reshape(g.tiles * block, LANES)

        def one_row(r, carry):
            for c in range(g.tiles):
                target[r, :, lane(c)] = flat[pl.ds(c * block + r, g.sub, stride=g.rows), :]
            return carry

        lax.fori_loop(0, g.rows, one_row, 0, unroll=2)

    gather_rows(s_uv, uv)
    gather_rows(s_hh, hh)
    top = top_half(g)
    n = g.halo
    sides = ((up, late_up, g.rows - n, g.rows - g.margin), (down, late_down, 0, 0))
    for out, late, start, edge in sides:
        for c in range(g.tiles):
            for i in range(n):
                out[i, :, lane(c)] = uv[start + i, :, lane(c)]
            for i in range(n // 2):
                out[n + i, :, lane(c)] = jnp.where(
                    top, hh[start + 2 * i, :, lane(c)], hh[start + 2 * i + 1, :, lane(c)])
            span = pl.ds(edge, g.margin)
            out[n + n // 2, :, lane(c)] = own_metric[span, lane(c)]
            out[n + n // 2 + 1, :, lane(c)] = own_active[span, lane(c)]
    for one in others:
        one.wait()
    gather_rows(s_qq, qq)
    for out, late, start, edge in sides:
        for c in range(g.tiles):
            for i in range(n):
                late[i, :, lane(c)] = qq[start + i, :, lane(c)]
            late[n, :, lane(c)] = s_geopot[pl.ds(edge, g.margin), lane(c)]
    for k in range(g.levels):
        jumps[k] = jnp.full((g.sub, LANES), s_theta[k], jnp.float32)


def chip_mass_kernel(g, mass, other, total):
    for c in range(g.tiles):
        value = mass[:, lane(c)]
        for k in range(g.layers):
            value = value + jnp.abs(other[k, :, lane(c)])
        total[:, lane(c)] = value


def switches(me):
    high = me // 2
    odd = me - 2 * high
    return [jnp.where(flag, 1.0, 0.0) for flag in (high == 1, high == 0, odd == 1, odd == 0)]


def exner_kernel(g, place, jumps, own, other, above, weighted, chip_sum):
    me = place[0]
    partner = me + 1 - 2 * lax.rem(me, 2)
    low_chip, high_chip, low_group, high_group = switches(me)
    kinds = g.rows // g.sub

    def group(field, owner, offset, c, r):
        running = offset
        terms = []
        for k in range(g.layers):
            running = running + jnp.abs(field[k, pl.ds(r * g.sub, g.sub), lane(c)])
            pressure = top_pressure + running * (1.0 / g.levels)
            terms.append(jumps[owner * g.layers + k] * jnp.exp(exner_power * jnp.log(pressure)))
        for k in range(g.layers - 2, -1, -1):
            terms[k] = terms[k] + terms[k + 1]
        return terms

    def size(field, c, r):
        total = jnp.abs(field[0, pl.ds(r * g.sub, g.sub), lane(c)])
        for k in range(1, g.layers):
            total = total + jnp.abs(field[k, pl.ds(r * g.sub, g.sub), lane(c)])
        return total

    for c in range(g.tiles):
        for r in range(kinds):
            rows = pl.ds(r * g.sub, g.sub)
            outer = above[rows, lane(c)] * low_chip
            mine = group(own, me, outer + size(other, c, r) * low_group, c, r)
            theirs = group(other, partner, outer + size(own, c, r) * high_group, c, r)
            for k in range(g.layers):
                weighted[k, rows, lane(c)] = mine[k] + theirs[0] * high_group
            chip_sum[rows, lane(c)] = mine[0] + theirs[0]


def montgomery_kernel(g, place, weighted, beneath, geopot, up, down, mm, s_mm):
    high_chip = switches(place[0])[1]
    block = g.sub * g.rows
    for c in range(g.tiles):
        base = beneath[:, lane(c)] * high_chip
        for k in range(g.layers):
            value = geopot[:, lane(c)] + (weighted[k, :, lane(c)] + base)
            s_mm[c, 0, k] = value
            s_mm[c, 1, k] = value
    flat = s_mm.reshape(g.tiles * block, LANES)

    def one_row(r, carry):
        for c in range(g.tiles):
            mm[r, :, lane(c)] = flat[pl.ds(c * block + r, g.sub, stride=g.rows), :]
        return carry

    lax.fori_loop(0, g.rows, one_row, 0, unroll=2)
    top = top_half(g)
    for out, start in ((up, g.rows - g.halo), (down, 0)):
        for c in range(g.tiles):
            for i in range(g.halo // 2):
                out[i, :, lane(c)] = jnp.where(
                    top, mm[start + 2 * i, :, lane(c)], mm[start + 2 * i + 1, :, lane(c)])


def unpack_pair(g, top, value):
    other = swap_halves(g, value)
    return jnp.where(top, value, other), jnp.where(top, other, value)


def signed_coriolis(g, c):
    column = (lax.broadcasted_iota(jnp.int32, (g.sub, LANES), 1) + c * LANES).astype(jnp.float32)
    f = 0.5 + column / g.columns
    return jnp.where(top_half(g), f, -f)


def over_rows(low, high, one_row):
    assert (high - low) % 2 == 0

    def turn(i, carry):
        one_row(low + 2 * i)
        one_row(low + 2 * i + 1)
        return carry

    lax.fori_loop(0, (high - low) // 2, turn, 0)


def advance(g, low, high, scale, uv, uv0, coefs, mass=None, tracer=None):
    top = top_half(g)
    carry_rows, turn_rows, shrink_rows, inverse_rows = coefs

    def put(target, e, c, value):
        if target is None:
            return
        if callable(target):
            target(e, c, value)
        else:
            target[e, :, lane(c)] = value

    def one_row(e):
        here = row_of(g, uv, e)
        if mass is not None:
            flux, hh0, uv_out, hh_out, flux_out = mass
            uv_columns = column_differences(g, here, False)
            flux_columns = column_differences(g, row_of(g, flux, e), False)
        if tracer is not None:
            qq, qq0, qq_out = tracer
            qq_columns = column_differences(g, row_of(g, qq, e), False)
        for c in range(g.tiles):
            swapped = swap_halves(g, here[c])
            east = jnp.where(top, here[c], swapped)
            north = jnp.where(top, swapped, here[c])
            along = carry_rows[e, :, lane(c)] * scale
            if tracer is not None:
                rows = qq[e + 1, :, lane(c)] - qq[e - 1, :, lane(c)]
                put(qq_out, e, c, qq0[e, :, lane(c)]
                    + along * (east * rows + north * qq_columns[c]))
            if mass is not None:
                rows = uv[e + 1, :, lane(c)] - uv[e - 1, :, lane(c)]
                uv_new = (uv0[e, :, lane(c)] + along * (east * rows + north * uv_columns[c])
                          + (turn_rows[e, :, lane(c)] * scale) * swapped)
                put(uv_out, e, c, uv_new)
                rows = flux[e + 1, :, lane(c)] - flux[e - 1, :, lane(c)]
                mixed = jnp.where(top, rows, flux_columns[c])
                hh_new = hh0[e, :, lane(c)] + (shrink_rows[e, :, lane(c)] * scale) * (
                    mixed + swap_halves(g, mixed))
                put(hh_out, e, c, hh_new)
                if flux_out is not None:
                    put(flux_out, e, c, hh_new * uv_new * inverse_rows[e, :, lane(c)])

    over_rows(low, high, one_row)


def fill_flux(g, low, high, uv, hh, inverse, flux):
    def one_row(e):
        for c in range(g.tiles):
            flux[e, :, lane(c)] = (
                hh[e, :, lane(c)] * uv[e, :, lane(c)] * inverse[e, :, lane(c)])

    over_rows(low, high, one_row)


def add_gradient(g, low, high, scale, mm, uv, hh, coefs, uv_out, pull, flux_out):
    top = top_half(g)
    carry_rows, turn_rows, shrink_rows, inverse_rows = coefs

    def one_row(e):
        columns = column_differences(g, row_of(g, mm, e), True)
        for c in range(g.tiles):
            gradient = jnp.where(
                top, mm[e + 1, :, lane(c)] - mm[e - 1, :, lane(c)], columns[c])
            force = carry_rows[e, :, lane(c)] * gradient
            value = uv[e, :, lane(c)] + scale * force
            uv_out[e, :, lane(c)] = value
            pull[e, :, lane(c)] = force
            flux_out[e, :, lane(c)] = (
                hh[e, :, lane(c)] * value * inverse_rows[e, :, lane(c)])

    over_rows(low, high, one_row)


def prepare_kernel(g, place, uv_own, hh_own, up, down, metric, active,
                   uv0, hh0, carry, turn, shrink, inverse, uv1, hh1,
                   flux, s_metric, s_active, sem):
    n = g.halo
    w = g.wide
    own = pl.ds(n, g.rows)
    copies = [
        pltpu.make_async_copy(uv_own, uv0.at[own], sem.at[0]),
        pltpu.make_async_copy(hh_own, hh0.at[own], sem.at[1]),
    ]
    for one in copies:
        one.start()
    top = top_half(g)
    low, high = pl.ds(0, g.margin), pl.ds(g.margin + g.rows, g.margin)
    own = pl.ds(g.margin, g.rows)
    m = n + n // 2
    for c in range(g.tiles):
        for span, value, count in (
            (low, up[m, :, lane(c)], up[m + 1, :, lane(c)]),
            (own, metric[:, lane(c)], active[:, lane(c)]),
            (high, down[m, :, lane(c)], down[m + 1, :, lane(c)]),
        ):
            s_metric[c, span] = value
            s_active[c, span] = count
    for halo, start in ((up, 0), (down, n + g.rows)):
        for c in range(g.tiles):
            for i in range(n):
                uv0[start + i, :, lane(c)] = halo[i, :, lane(c)]
            for i in range(n // 2):
                one, two = unpack_pair(g, top, halo[n + i, :, lane(c)])
                hh0[start + 2 * i, :, lane(c)] = one
                hh0[start + 2 * i + 1, :, lane(c)] = two
    layer = (place[0] * g.layers + lax.rem(sublane_index(g), g.layers)).astype(jnp.float32)
    metric_rows = s_metric.reshape(g.tiles * g.plane, LANES)
    active_rows = s_active.reshape(g.tiles * g.plane, LANES)
    shift = g.margin - n
    coriolis = [signed_coriolis(g, c) for c in range(g.tiles)]
    for one in copies:
        one.wait()

    def one_row(e):
        for c in range(g.tiles):
            value = spread(metric_rows, g.plane, c, e + shift)
            live = layer < spread(active_rows, g.plane, c, e + shift)
            along = jnp.where(live, -0.5 * value, 0.0)
            carry[e, :, lane(c)] = along
            shrink[e, :, lane(c)] = along * value
            turn[e, :, lane(c)] = jnp.where(live, coriolis[c], 0.0)
            one_over = 1.0 / value
            inverse[e, :, lane(c)] = one_over
            flux[e, :, lane(c)] = hh0[e, :, lane(c)] * uv0[e, :, lane(c)] * one_over

    over_rows(0, w, one_row)
    advance(g, 1, w - 1, time_step * FRACTIONS[0], uv0, uv0, (carry, turn, shrink, inverse),
            mass=(flux, hh0, uv1, hh1, None))


def with_pull(g, uv0, pull, scale):
    class Sum:
        def __getitem__(self, where):
            return uv0[where] + pull[where] * scale

    return Sum()


def first_kernel(g, uv0, hh0, carry, turn, shrink, inverse, uv1_part, hh1, mm_own, m_up, m_down,
                 uv1, uv2, uv3, hh3, sizes, mm, pull, flux0, flux1, sem):
    n = g.halo
    w = g.wide
    coefs = (carry, turn, shrink, inverse)
    copy = pltpu.make_async_copy(mm_own, mm.at[pl.ds(n, g.rows)], sem.at[0])
    copy.start()
    top = top_half(g)
    for halo, start in ((m_up, 0), (m_down, n + g.rows)):
        for c in range(g.tiles):
            for i in range(n // 2):
                one, two = unpack_pair(g, top, halo[i, :, lane(c)])
                mm[start + 2 * i, :, lane(c)] = one
                mm[start + 2 * i + 1, :, lane(c)] = two
    copy.wait()
    s = [time_step * fraction for fraction in FRACTIONS]
    add_gradient(g, 1, w - 1, s[0], mm, uv1_part, hh1, coefs, uv1, pull, flux1)
    advance(g, 2, w - 2, s[1], uv1, with_pull(g, uv0, pull, s[1]), coefs,
            mass=(flux1, hh0, uv2, None, flux0))
    advance(g, 3, w - 3, s[2], uv2, with_pull(g, uv0, pull, s[2]), coefs,
            mass=(flux0, hh0, uv3, hh3, None))
    first = len(FRACTIONS)
    for i in range((w - 2 * first) // 2):
        e = first + 2 * i
        for c in range(g.tiles):
            sizes[i, :, lane(c)] = jnp.abs(
                jnp.where(top, hh3[e, :, lane(c)], hh3[e + 1, :, lane(c)]))


def any_lane(c):
    return pl.ds(pl.multiple_of(c * LANES, LANES), LANES)


def suffix_sums(g, layer, value):
    value = value + jnp.where(layer < g.layers - 1, pltpu.roll(value, g.sub - 1, 0), 0.0)
    return value + jnp.where(layer < g.layers - 2, pltpu.roll(value, g.sub - 2, 0), 0.0)


def prefix_sums(g, layer, value):
    value = value + jnp.where(layer >= 1, pltpu.roll(value, 1, 0), 0.0)
    return value + jnp.where(layer >= 2, pltpu.roll(value, 2, 0), 0.0)


def place_rows(g, rows, place_in, j, value):
    rows = jnp.where(place_in == j, pltpu.roll(value, j, 0) if j else value, rows)
    return jnp.where(place_in == j + 1, pltpu.roll(value, (j + 1 - g.layers) % g.sub, 0), rows)


def second_mass_kernel(g, own, other, total):
    place_in = sublane_index(g)
    layer = lax.rem(place_in, g.layers)
    pairs = own.shape[0]

    def one_tile(c, carry):
        for start in range(0, total.shape[0], g.sub):
            rows = jnp.zeros((g.sub, LANES), jnp.float32)
            for j in range(0, g.sub, 2):
                i = (start + j) // 2
                if i < pairs:
                    value = own[i, :, any_lane(c)] + other[i, :, any_lane(c)]
                    rows = place_rows(g, rows, place_in, j, suffix_sums(g, layer, value))
            total[pl.ds(start, g.sub), any_lane(c)] = rows
        return carry

    lax.fori_loop(0, g.tiles, one_tile, 0)


def spread_total(g, layer, prefix):
    value = jnp.where(layer == g.layers - 1, prefix, 0.0)
    value = value + jnp.where(layer < g.layers - 1, pltpu.roll(value, g.sub - 1, 0), 0.0)
    return value + jnp.where(layer < g.layers - 2, pltpu.roll(value, g.sub - 2, 0), 0.0)


def spread_first(g, layer, suffix):
    value = jnp.where(layer == 0, suffix, 0.0)
    value = value + jnp.where(layer == 1, pltpu.roll(value, 1, 0), 0.0)
    return value + jnp.where(layer >= 2, pltpu.roll(value, 2, 0), 0.0)


def second_exner_kernel(g, place, jumps, own, other, above, weighted, chip_sum, s_above):
    me = place[0]
    partner = me + 1 - 2 * lax.rem(me, 2)
    low_chip, high_chip, low_group, high_group = switches(me)
    height = s_above.shape[1]
    for c in range(g.tiles):
        s_above[c] = above[:, lane(c)] * low_chip
    flat = s_above.reshape(g.tiles * height, LANES)
    place_in = sublane_index(g)
    layer = lax.rem(place_in, g.layers)
    top = top_half(g)

    def jump_of(owner):
        value = jumps[owner * g.layers]
        for k in range(1, g.layers):
            value = jnp.where(layer == k, jumps[owner * g.layers + k], value)
        return value

    my_jump, their_jump = jump_of(me), jump_of(partner)
    pairs = own.shape[0]

    def terms(prefix, jump):
        pressure = top_pressure + prefix * (1.0 / g.levels)
        return suffix_sums(g, layer, jump * jnp.exp(exner_power * jnp.log(pressure)))

    def one_tile(c, carry):
        for start in range(0, height, g.sub):
            rows = jnp.zeros((g.sub, LANES), jnp.float32)
            for j in range(0, g.sub, 2):
                i = (start + j) // 2
                if i >= pairs:
                    continue
                mine = prefix_sums(g, layer, own[i, :, any_lane(c)])
                theirs = prefix_sums(g, layer, other[i, :, any_lane(c)])
                outer = jnp.where(top, spread(flat, height, c, 2 * i),
                                  spread(flat, height, c, 2 * i + 1))
                my_terms = terms(
                    mine + outer + spread_total(g, layer, theirs) * low_group, my_jump)
                their_terms = terms(
                    theirs + outer + spread_total(g, layer, mine) * high_group, their_jump)
                weighted[i, :, any_lane(c)] = (
                    my_terms + spread_first(g, layer, their_terms) * high_group)
                rows = place_rows(g, rows, place_in, j, my_terms + their_terms)
            chip_sum[pl.ds(start, g.sub), any_lane(c)] = rows
        return carry

    lax.fori_loop(0, g.tiles, one_tile, 0)


def tracer_kernel(g, late_up, late_down, qq_own, uv0, uv1, uv2, carry, qq3, qq0, qq1, qq2, sem):
    n = g.halo
    w = g.wide
    copy = pltpu.make_async_copy(qq_own, qq0.at[pl.ds(n, g.rows)], sem.at[0])
    copy.start()
    for halo, start in ((late_up, 0), (late_down, n + g.rows)):
        for c in range(g.tiles):
            for i in range(n):
                qq0[start + i, :, lane(c)] = halo[i, :, lane(c)]
    copy.wait()
    s = [time_step * fraction for fraction in FRACTIONS]
    coefs = (carry, None, None, None)
    advance(g, 1, w - 1, s[0], uv0, None, coefs, tracer=(qq0, qq0, qq1))
    advance(g, 2, w - 2, s[1], uv1, None, coefs, tracer=(qq1, qq0, qq2))
    advance(g, 3, w - 3, s[2], uv2, None, coefs, tracer=(qq2, qq0, qq3))


def again_kernel(g, uv3, hh3, carry, turn, shrink, inverse, uv4, hh4, flux):
    first = len(FRACTIONS)
    w = g.wide
    fill_flux(g, first, w - first, uv3, hh3, inverse, flux)
    advance(g, first + 1, w - first - 1, time_step * FRACTIONS[0], uv3, uv3,
            (carry, turn, shrink, inverse), mass=(flux, hh3, uv4, hh4, None))


def last_kernel(g, place, weighted, beneath, geopot, late_up, late_down,
                uv3, hh3, qq3, carry, turn, shrink, inverse, uv4_part, hh4,
                u_out, v_out, h_out, q1_out, q2_out,
                mm, pull, uv4, uv5, flux0, flux1, qq4, qq5, s_geopot, s_beneath,
                s_uv, s_hh, s_qq, sem):
    n = g.halo
    first = len(FRACTIONS)
    w = g.wide
    s = [time_step * fraction for fraction in FRACTIONS]
    coefs = (carry, turn, shrink, inverse)
    top = top_half(g)
    high_chip = switches(place[0])[1]
    height = s_beneath.shape[1]
    for c in range(g.tiles):
        s_geopot[c, pl.ds(0, g.margin)] = late_up[n, :, lane(c)]
        s_geopot[c, pl.ds(g.margin, g.rows)] = geopot[:, lane(c)]
        s_geopot[c, pl.ds(g.margin + g.rows, g.margin)] = late_down[n, :, lane(c)]
        s_beneath[c] = beneath[:, lane(c)] * high_chip
    geopot_rows = s_geopot.reshape(g.tiles * g.plane, LANES)
    beneath_rows = s_beneath.reshape(g.tiles * height, LANES)
    shift = g.margin - n

    def one_pair(i, carried):
        e = first + 2 * i
        for c in range(g.tiles):
            base = jnp.where(top, spread(geopot_rows, g.plane, c, e + shift),
                             spread(geopot_rows, g.plane, c, e + 1 + shift))
            offset = jnp.where(top, spread(beneath_rows, height, c, 2 * i),
                               spread(beneath_rows, height, c, 2 * i + 1))
            one, two = unpack_pair(g, top, base + (weighted[i, :, lane(c)] + offset))
            mm[e, :, lane(c)] = one
            mm[e + 1, :, lane(c)] = two
        return carried

    lax.fori_loop(0, (w - 2 * first) // 2, one_pair, 0)
    add_gradient(g, first + 1, w - first - 1, s[0], mm, uv4_part, hh4, coefs, uv4, pull, flux1)
    advance(g, 4, w - 4, s[0], uv3, None, coefs, tracer=(qq3, qq3, qq4))
    advance(g, 5, w - 5, s[1], uv4, with_pull(g, uv3, pull, s[1]), coefs,
            mass=(flux1, hh3, uv5, None, flux0), tracer=(qq4, qq3, qq5))
    block = g.sub * g.rows

    def store_in(scratch):
        flat = scratch.reshape(g.tiles * block, LANES)

        def store(e, c, value):
            flat[pl.ds(c * block + e - n, g.sub, stride=g.rows), :] = value

        return store

    advance(g, 6, w - 6, s[2], uv5, with_pull(g, uv3, pull, s[2]), coefs,
            mass=(flux0, hh3, store_in(s_uv), store_in(s_hh), None),
            tracer=(qq5, qq3, store_in(s_qq)))
    copies = []
    for target, scratch, slot in ((u_out, s_uv, 0), (v_out, s_uv, 1), (h_out, s_hh, 0),
                                  (q1_out, s_qq, 0), (q2_out, s_qq, 1)):
        for c in range(g.tiles):
            copies.append(pltpu.make_async_copy(
                scratch.at[c, slot], target.at[:, :, lane(c)], sem.at[0]))
    for one in copies:
        one.start()
    for one in copies:
        one.wait()


def local(
    wind_east,
    wind_north,
    thickness,
    tracer_one,
    tracer_two,
    theta_step,
    surface_geopot,
    map_factor,
    active_layers,
):
    layers, rows, columns = thickness.shape
    groups = lax.axis_size("lev")
    assert groups == 4
    g = Geometry(layers, rows, columns, layers * groups)
    n, w = g.halo, g.wide
    first = len(FRACTIONS)
    pairs = (w - 2 * first) // 2
    height = -(-2 * pairs // 8) * 8
    count = lax.axis_size("row")
    forward = [(i, (i + 1) % count) for i in range(count)]
    backward = [(i, (i - 1) % count) for i in range(count)]
    on_chip = [(i, i ^ 1) for i in range(groups)]
    over_chips = [(i, i ^ 2) for i in range(groups)]
    place = lax.axis_index("lev").astype(jnp.int32).reshape(1)

    def shape(*dims):
        return pltpu.VMEM(dims, jnp.float32)

    def move(value, axis, pairs_of):
        return pltpu.with_memory_space_constraint(
            lax.ppermute(value, axis, pairs_of), pltpu.VMEM)

    def call(body, outs, ins, scratch, name, out_specs=None):
        return pl.pallas_call(
            functools.partial(body, g),
            out_shape=outs,
            in_specs=ins,
            out_specs=out_specs if out_specs is not None else [VMEM] * len(outs),
            scratch_shapes=scratch,
            compiler_params=pltpu.CompilerParams(vmem_limit_bytes=SCOPED_BYTES),
            name=name,
        )

    slab = shape(rows, g.sub, columns)
    broad = shape(w, g.sub, columns)
    flat = shape(rows, columns)
    plane_out = shape(height, columns)
    stack = shape(pairs, g.sub, columns)
    fields = pltpu.VMEM((g.tiles, 2, layers, rows, LANES), jnp.float32)
    plane = pltpu.VMEM((g.tiles, g.plane, LANES), jnp.float32)
    offsets = pltpu.VMEM((g.tiles, height, LANES), jnp.float32)
    dma = pltpu.SemaphoreType.DMA
    early = n + n // 2 + 2

    other_h = move(thickness, "lev", on_chip)
    (up, down, late_up, late_down, uv, hh, qq, mass, metric, active, jumps) = call(
        pack_kernel,
        [shape(early, g.sub, columns)] * 2 + [shape(n + 1, g.sub, columns)] * 2
        + [slab] * 3 + [flat] * 3 + [shape(g.levels, g.sub, LANES)],
        [FAR] * 9,
        [fields] * 3 + [pltpu.VMEM((rows, columns), jnp.int32), flat,
                        pltpu.SMEM((g.levels,), jnp.float32), dma((3,))],
        "pack",
    )(*(pltpu.with_memory_space_constraint(value, pltpu.HBM) for value in (
        wind_east, wind_north, thickness, tracer_one, tracer_two,
        map_factor, active_layers, surface_geopot, theta_step)))
    (total,) = call(chip_mass_kernel, [flat], [VMEM] * 2, [], "chip_mass")(mass, other_h)
    up_in = move(up, "row", forward)
    down_in = move(down, "row", backward)
    weighted, chip_sum = call(
        exner_kernel, [shape(layers, rows, columns), flat], [SMEM] + [VMEM] * 4, [], "exner",
    )(place, jumps, thickness, other_h, move(total, "lev", over_chips))
    m_up, m_down, mm = call(
        montgomery_kernel, [shape(n // 2, g.sub, columns)] * 2 + [slab],
        [SMEM] + [VMEM] * 3, [fields], "montgomery",
    )(place, weighted, move(chip_sum, "lev", over_chips), surface_geopot)
    m_up_in = move(m_up, "row", forward)
    m_down_in = move(m_down, "row", backward)
    uv0, hh0, carry, turn, shrink, inverse, uv1_part, hh1 = call(
        prepare_kernel, [broad] * 8, [SMEM] + [VMEM] * 6,
        [broad] + [plane] * 2 + [dma((2,))], "prepare",
    )(place, uv, hh, up_in, down_in, metric, active)
    uv1, uv2, uv3, hh3, sizes = call(
        first_kernel, [broad] * 4 + [stack], [VMEM] * 11, [broad] * 4 + [dma((1,))], "first",
    )(uv0, hh0, carry, turn, shrink, inverse, uv1_part, hh1, mm, m_up_in, m_down_in)
    late_up_in = move(late_up, "row", forward)
    late_down_in = move(late_down, "row", backward)
    other_sizes = move(sizes, "lev", on_chip)
    (total,) = call(second_mass_kernel, [plane_out], [VMEM] * 2, [], "second_mass")(
        sizes, other_sizes)
    uv4_part, hh4 = call(again_kernel, [broad] * 2, [VMEM] * 6, [broad], "again")(
        uv3, hh3, carry, turn, shrink, inverse)
    weighted, chip_sum = call(
        second_exner_kernel, [stack, plane_out], [SMEM] + [VMEM] * 4, [offsets], "second_exner",
    )(place, jumps, sizes, other_sizes, move(total, "lev", over_chips))
    (qq3,) = call(
        tracer_kernel, [broad], [VMEM] * 7, [broad] * 3 + [dma((1,))], "tracer",
    )(late_up_in, late_down_in, qq, uv0, uv1, uv2, carry)
    return tuple(call(
        last_kernel, [jax.ShapeDtypeStruct((layers, rows, columns), jnp.float32)] * 5,
        [SMEM] + [VMEM] * 14,
        [broad] * 8 + [plane, offsets] + [fields] * 3 + [dma((1,))],
        "last", [FAR] * 5,
    )(place, weighted, move(chip_sum, "lev", over_chips), surface_geopot, late_up_in,
      late_down_in, uv3, hh3, qq3, carry, turn, shrink, inverse, uv4_part, hh4))


def solution(mesh):
    state = P("lev", "row", None)
    flat = P("row", None)
    return jax.shard_map(
        local,
        mesh=mesh,
        in_specs=(state,) * 5 + (P(), flat, flat, flat),
        out_specs=(state,) * 5,
        check_vma=False,
    )
```

time: 83.5 us -> 60.5 us (0.72); the launches traced: 82.2 us -> 60.3 us
  blocking collectives: 24.9 us -> 0 us
  starting transfers between devices: 12.5 us -> 22.3 us
  waiting for transfers between devices: 3.03 us -> 12.5 us
  local copies, waits for them, and re-layouts: 9.31 us -> 0.71 us
  Pallas kernels: 31.7 us -> 24.1 us
    all_gather x4 -> x0, blocking collectives: 24.9 us -> none  [the longest x2 12.6 us: local(): lax.all_gather(below, 'lev')]
    ppermute x6 -> x12, starting transfers between devices: 12.5 us -> 22.3 us  [move(): lax.ppermute(value, axis, pairs_of)]
    ppermute x6 -> x12, waiting for transfers between devices: 3.03 us -> 12.5 us  [move(): lax.ppermute(value, axis, pairs_of)]
    pallas_call x4 -> x9, Pallas kernels: 29.9 us -> 21.1 us  [the longest x1 6.72 us: local(): call(last_kernel, [jax.ShapeDtypeStruct((layers, rows, columns), jnp.floa...]
    unnamed x34 -> x12, local copies, waits for them, and re-layouts: 9.31 us -> 0.71 us
    pallas_call x1, Pallas kernels: 1.42 us -> 2.73 us  [local(): call(pack_kernel, [shape(early, g.sub, columns)] * 2 + [shape(n + 1, g.su...]
  transfers between devices with their start and end apart: 6 -> 12, of which waited for: 1 -> 5; matrix products, arithmetic and copies ran while one was open for 0% -> 0% of each run, Pallas kernels for 16% -> 21%
where the time goes in v3:
time: 60.5 us; the launch traced here: 60.3 us
  Pallas kernels  24.1 us (40%)
  starting transfers between devices  22.3 us (37%)
  waiting for transfers between devices  12.5 us (21%)
  between operations  0.79 us (1%)
  local copies, waits for them, and re-layouts  0.71 us (1%)
    ppermute x12, starting transfers between devices, move(): lax.ppermute(value, axis, pairs_of)  22.3 us
    ppermute x12, waiting for transfers between devices, move(): lax.ppermute(value, axis, pairs_of)  12.5 us
    pallas_call x1, Pallas kernels, local(): call(last_kernel, [jax.ShapeDtypeStruct((layers, rows, columns), jnp.floa...  6.72 us
    pallas_call x1, Pallas kernels, local(): call(first_kernel, [broad] * 4 + [stack], [VMEM] * 11, [broad] * 4 + [dma...  4.87 us
    pallas_call x1, Pallas kernels, local(): call(tracer_kernel, [broad], [VMEM] * 7, [broad] * 3 + [dma((1,))], 'trac...  3.96 us
    pallas_call x1, Pallas kernels, local(): call(pack_kernel, [shape(early, g.sub, columns)] * 2 + [shape(n + 1, g.su...  2.73 us
    pallas_call x1, Pallas kernels, local(): call(prepare_kernel, [broad] * 8, [SMEM] + [VMEM] * 6, [broad] + [plane]...  2.4 us
    pallas_call x1, Pallas kernels, local(): call(again_kernel, [broad] * 2, [VMEM] * 6, [broad], 'again')  1.56 us
  transfers between devices with their start and end apart: 12, of which 5 were waited for; matrix products, arithmetic and copies ran while one was open for 0% of the time, Pallas kernels for 21%

profile of v3, /device:TPU:0, one launch (start us, length us, event | category | flops | bytes accessed | tf_op | source)
XLA Modules:
  0.0 60.3 jit_solution(10711557907958336686)
XLA Ops:
  0.6 0.6 collective-permute-start.2
  1.2 2.7 %pack.1 = (f32[11,8,1024]{2,1,0:T(8,128)}, f32[11,8,1024]{2,1,0:T(8,128)S(1)}, f32[7,8,1024]{2,1,0:T(8,128)S(1)}, f32[7,8,1024]{2,1,0:T(8,128)S(1)}, f32[16,8,10...) custom-call(f32[4,16,1024]{2,1,0:T(8,128)} %u.1, ...), custom_call_target="tpu_custom_call" | custom-call | tf_op jit(solution)/shard_map/pack/pallas_call | solution.py:652
  3.9 0.0 copy-start.4
  3.9 0.7 %copy-done.4 = f32[7,8,1024]{2,1,0:T(8,128)} copy-done((f32[7,8,1024]{2,1,0:T(8,128)}, f32[7,8,1024]{2,1,0:T(8,128)S(1)}, u32[]{:S(2)}) %copy-start.4) | copy-done | bytes 229400
  4.6 0.0 copy-start.2
  4.6 0.0 copy-start
  4.6 2.5 %collective-permute-start = (f32[11,8,1024]{2,1,0:T(8,128)}, f32[11,8,1024]{2,1,0:T(8,128)S(1)}, u32[]{:S(2)}, u32[]{:S(2)}) collective-permute-start(f32[11,8,1024]{2,1,0:T(8,128)} %get-tuple-element.41), channel_id=1, source_target_pairs={{0,1},{1,2},{2,3},{3,4},{4,5},{5,6},{6,7},{7,0},{8,9},{9,10},{10,1... | collective-permute-start | bytes 1081352 | tf_op jit(solution)/shard_map/ppermute | solution.py:627
  7.2 3.0 %collective-permute-start.1 = (f32[11,8,1024]{2,1,0:T(8,128)S(1)}, f32[11,8,1024]{2,1,0:T(8,128)S(1)}, u32[]{:S(2)}, u32[]{:S(2)}) collective-permute-start(f32[11,8,1024]{2,1,0:T(8,128)S(1)} %get-tuple-element.42), channel_id=1, source_target_pairs={{0,7},{1,0},{2,1},{3,2},{4,3},{5,4},{6,5},{7,6},{8,15},{9,8},{10,9... | collective-permute-start | bytes 1081352 | tf_op jit(solution)/shard_map/ppermute | solution.py:627
  10.2 0.0 collective-permute-done.2.other
  10.2 1.7 %collective-permute-start.3 = (f32[16,1024]{1,0:T(8,128)S(1)}, f32[16,1024]{1,0:T(8,128)S(1)}, u32[]{:S(2)}, u32[]{:S(2)}) collective-permute-start(f32[16,1024]{1,0:T(8,128)S(1)} %chip_mass.1), channel_id=1, source_target_pairs={{0,16},{8,24},{16,0},{24,8},{1,17},{9,25},{17,1},{25,9},{2,18},{10... | collective-permute-start | bytes 196616 | tf_op jit(solution)/shard_map/ppermute | solution.py:627
  12.0 0.0 copy-done.2
  12.0 2.6 %collective-permute-done.3.above = f32[16,1024]{1,0:T(8,128)S(1)} collective-permute-done((f32[16,1024]{1,0:T(8,128)S(1)}, f32[16,1024]{1,0:T(8,128)S(1)}, u32[]{:S(2)}, u32[]{:S(2)}) %collective-permute-start.3) | collective-permute-done | bytes 65568 | tf_op jit(solution)/shard_map/ppermute | solution.py:627
  14.6 0.0 copy-done
  14.6 0.0 copy-start.1
  14.6 0.2 exner.1
  14.8 1.7 %collective-permute-start.4 = (f32[16,1024]{1,0:T(8,128)S(1)}, f32[16,1024]{1,0:T(8,128)S(1)}, u32[]{:S(2)}, u32[]{:S(2)}) collective-permute-start(f32[16,1024]{1,0:T(8,128)S(1)} %get-tuple-element.55), channel_id=1, source_target_pairs={{0,16},{8,24},{16,0},{24,8},{1,17},{9,25},{17,1},{25,9},{2,18},{10... | collective-permute-start | bytes 196616 | tf_op jit(solution)/shard_map/ppermute | solution.py:627
  16.5 2.6 %collective-permute-done.4.beneath = f32[16,1024]{1,0:T(8,128)S(1)} collective-permute-done((f32[16,1024]{1,0:T(8,128)S(1)}, f32[16,1024]{1,0:T(8,128)S(1)}, u32[]{:S(2)}, u32[]{:S(2)}) %collective-permute-start.4) | collective-permute-done | bytes 65568 | tf_op jit(solution)/shard_map/ppermute | solution.py:627
  19.1 0.0 copy-done.1
  19.1 0.3 montgomery.1
  19.4 0.1 collective-permute-start.5
  19.5 4.7 %collective-permute-start.6 = (f32[3,8,1024]{2,1,0:T(8,128)S(1)}, f32[3,8,1024]{2,1,0:T(8,128)S(1)}, u32[]{:S(2)}, u32[]{:S(2)}) collective-permute-start(f32[3,8,1024]{2,1,0:T(8,128)S(1)} %get-tuple-element.58), channel_id=1, source_target_pairs={{0,7},{1,0},{2,1},{3,2},{4,3},{5,4},{6,5},{7,6},{8,15},{9,8},{10,9... | collective-permute-start | bytes 294920 | tf_op jit(solution)/shard_map/ppermute | solution.py:627
  24.2 1.9 %collective-permute-done.up = f32[11,8,1024]{2,1,0:T(8,128)S(1)} collective-permute-done((f32[11,8,1024]{2,1,0:T(8,128)}, f32[11,8,1024]{2,1,0:T(8,128)S(1)}, u32[]{:S(2)}, u32[]{:S(2)}) %collective-permute-start) | collective-permute-done | bytes 360480 | tf_op jit(solution)/shard_map/ppermute | solution.py:627
  26.1 2.2 %collective-permute-done.1.down = f32[11,8,1024]{2,1,0:T(8,128)S(1)} collective-permute-done((f32[11,8,1024]{2,1,0:T(8,128)S(1)}, f32[11,8,1024]{2,1,0:T(8,128)S(1)}, u32[]{:S(2)}, u32[]{:S(2)}) %collective-permute-start.1) | collective-permute-done | bytes 360480 | tf_op jit(solution)/shard_map/ppermute | solution.py:627
  28.3 2.4 %prepare.1 = (f32[28,8,1024]{2,1,0:T(8,128)S(1)}, f32[28,8,1024]{2,1,0:T(8,128)S(1)}, f32[28,8,1024]{2,1,0:T(8,128)S(1)}, f32[28,8,1024]{2,1,0:T(8,128)S(1)}, f3...) custom-call(s32[1]{0:T(128)} %bitcast.place, ...), custom_call_target="tpu_custom_call" | custom-call | tf_op jit(solution)/shard_map/prepare/pallas_call | solution.py:675
  30.7 0.0 collective-permute-done.5.m_up
  30.7 0.0 collective-permute-done.6.m_down
  30.7 0.0 copy-start.5
  30.7 0.0 copy-start.3
  30.7 4.9 %first.1 = (f32[28,8,1024]{2,1,0:T(8,128)S(1)}, f32[28,8,1024]{2,1,0:T(8,128)S(1)}, f32[28,8,1024]{2,1,0:T(8,128)S(1)}, f32[28,8,1024]{2,1,0:T(8,128)S(1)}, f32[11,8,1024]{2,1,0:T(8,128)S(1)}) custom-call(f32[28,8,1024]{2,1,0:T(8,128)S(1)} %get-tuple-element.45.uv0, f32[28,8,1024]{2,1,0:T(8,128)S(1)} %get-tuple-element.46.hh0, ...), custom_call_target="tpu_custom_call" | custom-call | tf_op jit(solution)/shard_map/first/pallas_call | solution.py:679
  35.6 0.1 collective-permute-start.7
  35.7 0.0 copy-done.5
  35.7 0.3 collective-permute-start.10
  36.0 0.0 copy-done.3
  36.0 4.5 %collective-permute-start.11 = (f32[7,8,1024]{2,1,0:T(8,128)S(1)}, f32[7,8,1024]{2,1,0:T(8,128)S(1)}, u32[]{:S(2)}, u32[]{:S(2)}) collective-permute-start(f32[7,8,1024]{2,1,0:T(8,128)S(1)} %copy-done.3), channel_id=1, source_target_pairs={{0,7},{1,0},{2,1},{3,2},{4,3},{5,4},{6,5},{7,6},{8,15},{9,8},{10,9... | collective-permute-start | bytes 688136 | tf_op jit(solution)/shard_map/ppermute | solution.py:627
  40.5 0.0 collective-permute-done.7.other
  40.5 0.2 second_mass.1
  40.7 1.6 %collective-permute-start.8 = (f32[24,1024]{1,0:T(8,128)S(1)}, f32[24,1024]{1,0:T(8,128)S(1)}, u32[]{:S(2)}, u32[]{:S(2)}) collective-permute-start(f32[24,1024]{1,0:T(8,128)S(1)} %second_mass.1), channel_id=1, source_target_pairs={{0,16},{8,24},{16,0},{24,8},{1,17},{9,25},{17,1},{25,9},{2,18},{10... | collective-permute-start | bytes 294920 | tf_op jit(solution)/shard_map/ppermute | solution.py:627
  42.3 3.1 %collective-permute-done.8.above = f32[24,1024]{1,0:T(8,128)S(1)} collective-permute-done((f32[24,1024]{1,0:T(8,128)S(1)}, f32[24,1024]{1,0:T(8,128)S(1)}, u32[]{:S(2)}, u32[]{:S(2)}) %collective-permute-start.8) | collective-permute-done | bytes 98336 | tf_op jit(solution)/shard_map/ppermute | solution.py:627
  45.4 1.1 %second_exner.1 = (f32[11,8,1024]{2,1,0:T(8,128)S(1)}, f32[24,1024]{1,0:T(8,128)S(1)}) custom-call(s32[1]{0:T(128)} %bitcast.place, f32[16,8,128]{2,1,0:T(8,128)S(1)} %get-tuple-element.38.jumps, f32[11,8,1024]{2,1,0:T(8,128)S(1)} %get-tuple-element.59.own, f32[11,8,1024]{2,1,0:T(8,128)S(1)} %collective-permute-done.7.other, ...), custom_call_target="tpu_custom_call" | custom-call | tf_op jit(solution)/shard_map/second_exner/pallas_call | solution.py:689
  46.5 1.6 %collective-permute-start.9 = (f32[24,1024]{1,0:T(8,128)S(1)}, f32[24,1024]{1,0:T(8,128)S(1)}, u32[]{:S(2)}, u32[]{:S(2)}) collective-permute-start(f32[24,1024]{1,0:T(8,128)S(1)} %get-tuple-element.61), channel_id=1, source_target_pairs={{0,16},{8,24},{16,0},{24,8},{1,17},{9,25},{17,1},{25,9},{2,18},{10... | collective-permute-start | bytes 294920 | tf_op jit(solution)/shard_map/ppermute | solution.py:627
  48.0 1.6 %again.1 = (f32[28,8,1024]{2,1,0:T(8,128)S(1)}, f32[28,8,1024]{2,1,0:T(8,128)S(1)}) custom-call(f32[28,8,1024]{2,1,0:T(8,128)S(1)} %get-tuple-element.64.uv3, f32[28,8,1024]{2,1,0:T(8,128)S(1)} %get-tuple-element.65.hh3, f32[28,8,1024]{2,1,0:T(8,128)S(1)} %get-tuple-element.47.carry, f32[28,8,1024]{2,1,0:T(8,128)S(1)} %get-tuple-element.48.turn, ...), custom_call_target="tpu_custom_call" | custom-call | tf_op jit(solution)/shard_map/again/pallas_call | solution.py:687
  49.6 0.0 collective-permute-done.10.late_up
  49.6 0.0 collective-permute-done.11.late_down
  49.6 4.0 %tracer.1.qq3 = f32[28,8,1024]{2,1,0:T(8,128)S(1)} custom-call(f32[7,8,1024]{2,1,0:T(8,128)S(1)} %collective-permute-done.10.late_up, f32[7,8,1024]{2,1,0:T(8,128)S(1)} %collective-permute-done.11.late_down, f32[16,8,1024]{2,1,0:T(8,128)S(1)} %get-tuple-element.66.qq_own, f32[28,8,1024]{2,1,0:T(8,128)S(1)} %get-tuple-element.45.uv0, ...), custom_call_target="tpu_custom_call" | custom-call | tf_op jit(solution)/shard_map/tracer/pallas_call | solution.py:692
  53.6 0.0 collective-permute-done.9.beneath
  53.6 6.7 %last.1 = (f32[4,16,1024]{2,1,0:T(8,128)}, f32[4,16,1024]{2,1,0:T(8,128)}, f32[4,16,1024]{2,1,0:T(8,128)}, f32[4,16,1024]{2,1,0:T(8,128)}, f32[4,16,1024]{2,1,0:T(8,128)}) custom-call(s32[1]{0:T(128)} %bitcast.place, f32[11,8,1024]{2,1,0:T(8,128)S(1)} %get-tuple-element.60.weighted, f32[24,1024]{1,0:T(8,128)S(1)} %collective-permute-done.9.beneath, ...), custom_call_target="tpu_custom_call" | custom-call | tf_op jit(solution)/shard_map/last/pallas_call | solution.py:695
  (1 shorter events, 0.0 us)
Async XLA Ops:
  0.6 9.6 %collective-permute-start.2 = (f32[4,16,1024]{2,1,0:T(8,128)}, f32[4,16,1024]{2,1,0:T(8,128)S(1)}, u32[]{:S(2)}, u32[]{:S(2)}) collective-permute-start(f32[4,16,1024]{2,1,0:T(8,128)} %own.1), channel_id=1, source_target_pairs={{0,8},{8,0},{16,24},{24,16},{1,9},{9,1},{17,25},{25,17},{2,10},{10... | collective-permute-start | bytes 786440 | tf_op jit(solution)/shard_map/ppermute | solution.py:627
  3.9 0.7 %copy-start.4 = (f32[7,8,1024]{2,1,0:T(8,128)}, f32[7,8,1024]{2,1,0:T(8,128)S(1)}, u32[]{:S(2)}) copy-start(f32[7,8,1024]{2,1,0:T(8,128)S(1)} %get-tuple-element.62) | copy-start | bytes 688132
  4.6 7.3 %copy-start.2 = (f32[7,8,1024]{2,1,0:T(8,128)}, f32[7,8,1024]{2,1,0:T(8,128)S(1)}, u32[]{:S(2)}) copy-start(f32[7,8,1024]{2,1,0:T(8,128)S(1)} %get-tuple-element.63) | copy-start | bytes 688132
  4.6 9.9 %copy-start = (f32[4,16,1024]{2,1,0:T(8,128)S(1)}, f32[4,16,1024]{2,1,0:T(8,128)}, u32[]{:S(2)}) copy-start(f32[4,16,1024]{2,1,0:T(8,128)} %own.1) | copy-start | bytes 786436
  4.6 21.5 %collective-permute-start = (f32[11,8,1024]{2,1,0:T(8,128)}, f32[11,8,1024]{2,1,0:T(8,128)S(1)}, u32[]{:S(2)}, u32[]{:S(2)}) collective-permute-start(f32[11,8,1024]{2,1,0:T(8,128)} %get-tuple-element.41), channel_id=1, source_target_pairs={{0,1},{1,2},{2,3},{3,4},{4,5},{5,6},{6,7},{7,0},{8,9},{9,10},{10,1... | collective-permute-start | bytes 1081352 | tf_op jit(solution)/shard_map/ppermute | solution.py:627
  7.2 21.1 %collective-permute-start.1 = (f32[11,8,1024]{2,1,0:T(8,128)S(1)}, f32[11,8,1024]{2,1,0:T(8,128)S(1)}, u32[]{:S(2)}, u32[]{:S(2)}) collective-permute-start(f32[11,8,1024]{2,1,0:T(8,128)S(1)} %get-tuple-element.42), channel_id=1, source_target_pairs={{0,7},{1,0},{2,1},{3,2},{4,3},{5,4},{6,5},{7,6},{8,15},{9,8},{10,9... | collective-permute-start | bytes 1081352 | tf_op jit(solution)/shard_map/ppermute | solution.py:627
  10.2 4.3 %collective-permute-start.3 = (f32[16,1024]{1,0:T(8,128)S(1)}, f32[16,1024]{1,0:T(8,128)S(1)}, u32[]{:S(2)}, u32[]{:S(2)}) collective-permute-start(f32[16,1024]{1,0:T(8,128)S(1)} %chip_mass.1), channel_id=1, source_target_pairs={{0,16},{8,24},{16,0},{24,8},{1,17},{9,25},{17,1},{25,9},{2,18},{10... | collective-permute-start | bytes 196616 | tf_op jit(solution)/shard_map/ppermute | solution.py:627
  14.6 4.6 %copy-start.1 = (f32[16,1024]{1,0:T(8,128)S(1)}, f32[16,1024]{1,0:T(8,128)}, u32[]{:S(2)}) copy-start(f32[16,1024]{1,0:T(8,128)} %geopot.5) | copy-start | bytes 196612
  14.8 4.3 %collective-permute-start.4 = (f32[16,1024]{1,0:T(8,128)S(1)}, f32[16,1024]{1,0:T(8,128)S(1)}, u32[]{:S(2)}, u32[]{:S(2)}) collective-permute-start(f32[16,1024]{1,0:T(8,128)S(1)} %get-tuple-element.55), channel_id=1, source_target_pairs={{0,16},{8,24},{16,0},{24,8},{1,17},{9,25},{17,1},{25,9},{2,18},{10... | collective-permute-start | bytes 196616 | tf_op jit(solution)/shard_map/ppermute | solution.py:627
  19.4 11.3 %collective-permute-start.5 = (f32[3,8,1024]{2,1,0:T(8,128)S(1)}, f32[3,8,1024]{2,1,0:T(8,128)S(1)}, u32[]{:S(2)}, u32[]{:S(2)}) collective-permute-start(f32[3,8,1024]{2,1,0:T(8,128)S(1)} %get-tuple-element.57), channel_id=1, source_target_pairs={{0,1},{1,2},{2,3},{3,4},{4,5},{5,6},{6,7},{7,0},{8,9},{9,10},{10,1... | collective-permute-start | bytes 294920 | tf_op jit(solution)/shard_map/ppermute | solution.py:627
  19.5 11.2 %collective-permute-start.6 = (f32[3,8,1024]{2,1,0:T(8,128)S(1)}, f32[3,8,1024]{2,1,0:T(8,128)S(1)}, u32[]{:S(2)}, u32[]{:S(2)}) collective-permute-start(f32[3,8,1024]{2,1,0:T(8,128)S(1)} %get-tuple-element.58), channel_id=1, source_target_pairs={{0,7},{1,0},{2,1},{3,2},{4,3},{5,4},{6,5},{7,6},{8,15},{9,8},{10,9... | collective-permute-start | bytes 294920 | tf_op jit(solution)/shard_map/ppermute | solution.py:627
  30.7 5.0 %copy-start.5 = (f32[7,8,1024]{2,1,0:T(8,128)S(1)}, f32[7,8,1024]{2,1,0:T(8,128)}, u32[]{:S(2)}) copy-start(f32[7,8,1024]{2,1,0:T(8,128)} %copy-done.4) | copy-start | bytes 688132
  30.7 5.2 %copy-start.3 = (f32[7,8,1024]{2,1,0:T(8,128)S(1)}, f32[7,8,1024]{2,1,0:T(8,128)}, u32[]{:S(2)}) copy-start(f32[7,8,1024]{2,1,0:T(8,128)} %copy-done.2) | copy-start | bytes 688132
  35.6 4.9 %collective-permute-start.7 = (f32[11,8,1024]{2,1,0:T(8,128)S(1)}, f32[11,8,1024]{2,1,0:T(8,128)S(1)}, u32[]{:S(2)}, u32[]{:S(2)}) collective-permute-start(f32[11,8,1024]{2,1,0:T(8,128)S(1)} %get-tuple-element.59.own), channel_id=1, source_target_pairs={{0,8},{8,0},{16,24},{24,16},{1,9},{9,1},{17,25},{25,17},{2,10},{10... | collective-permute-start | bytes 1081352 | tf_op jit(solution)/shard_map/ppermute | solution.py:627
  35.7 13.9 %collective-permute-start.10 = (f32[7,8,1024]{2,1,0:T(8,128)S(1)}, f32[7,8,1024]{2,1,0:T(8,128)S(1)}, u32[]{:S(2)}, u32[]{:S(2)}) collective-permute-start(f32[7,8,1024]{2,1,0:T(8,128)S(1)} %copy-done.5), channel_id=1, source_target_pairs={{0,1},{1,2},{2,3},{3,4},{4,5},{5,6},{6,7},{7,0},{8,9},{9,10},{10,1... | collective-permute-start | bytes 688136 | tf_op jit(solution)/shard_map/ppermute | solution.py:627
  36.0 13.6 %collective-permute-start.11 = (f32[7,8,1024]{2,1,0:T(8,128)S(1)}, f32[7,8,1024]{2,1,0:T(8,128)S(1)}, u32[]{:S(2)}, u32[]{:S(2)}) collective-permute-start(f32[7,8,1024]{2,1,0:T(8,128)S(1)} %copy-done.3), channel_id=1, source_target_pairs={{0,7},{1,0},{2,1},{3,2},{4,3},{5,4},{6,5},{7,6},{8,15},{9,8},{10,9... | collective-permute-start | bytes 688136 | tf_op jit(solution)/shard_map/ppermute | solution.py:627
  40.7 4.7 %collective-permute-start.8 = (f32[24,1024]{1,0:T(8,128)S(1)}, f32[24,1024]{1,0:T(8,128)S(1)}, u32[]{:S(2)}, u32[]{:S(2)}) collective-permute-start(f32[24,1024]{1,0:T(8,128)S(1)} %second_mass.1), channel_id=1, source_target_pairs={{0,16},{8,24},{16,0},{24,8},{1,17},{9,25},{17,1},{25,9},{2,18},{10... | collective-permute-start | bytes 294920 | tf_op jit(solution)/shard_map/ppermute | solution.py:627
  46.5 7.1 %collective-permute-start.9 = (f32[24,1024]{1,0:T(8,128)S(1)}, f32[24,1024]{1,0:T(8,128)S(1)}, u32[]{:S(2)}, u32[]{:S(2)}) collective-permute-start(f32[24,1024]{1,0:T(8,128)S(1)} %get-tuple-element.61), channel_id=1, source_target_pairs={{0,16},{8,24},{16,0},{24,8},{1,17},{9,25},{17,1},{25,9},{2,18},{10... | collective-permute-start | bytes 294920 | tf_op jit(solution)/shard_map/ppermute | solution.py:627
